TPU v7x, 32 devices: a whole 2x2x4 slice. The times are simulated.
32 devices in a mesh: slab: 8 (over z, y), col: 4 (over x, core).
Axes of the slice: x: 2, y: 2, z: 4, core: 2. Of those that a mesh axis runs over, the one named last changes fastest.
Arguments:
- vectors: float32 [64, 8192], P('col', 'slab'), may hold values from -6 to 6
- residual_block: float32 [64, 8192], P('col', 'slab'), may hold values from -0.024 to 0.024
- diag_inverse: float32 [64, 128, 128], P('slab'), may hold values from -0.05 to 1.06
- factor_blocks: float32 [64, 2, 128, 128], P('slab'), may hold values from -0.55 to 0.05
- band_diag: float32 [64, 128, 128], P('slab'), may hold values from -0.45 to 4.45
- band_off: float32 [64, 2, 128, 128], P('slab'), may hold values from -0.65 to 0.15
- band_offsets: int32 [64, 2], P('slab'), may hold values from 1 to 3, as said below
Outputs:
- preconditioned: float32 [64, 8192], P('col', 'slab')
- image: float32 [2, 64, 8192], P(None, 'col', 'slab')
- gram: float32 [2, 2, 64, 2, 64], P(None, None, 'col')
Inputs may be any that keep to these rules, and one draw needn't show every extreme that they name: `band_offsets`: each block row's 2 offsets are distinct and increasing.
All inputs are finite; a program needn't handle non-finite values.
Results may differ from a plain program's by a relative error of at most 0.0003.
Values sent between devices are 32-bit elements; how exact they have to be, the bound alone decides.
No kernel may reach another device: no remote copies, remote signals or barrier semaphores. Data moves between devices by JAX's collectives and lax.ppermute only.
A program may use at most 320 MiB of HBM per device.

v0:
```python
import functools

import jax
import jax.numpy as jnp
from jax import lax
from jax.experimental import pallas as pl
from jax.experimental.pallas import tpu as pltpu
from jax.sharding import PartitionSpec as P


BS = 128
BW = 3
TAIL = BW * BS
BF = jnp.bfloat16
F32 = jnp.float32
NN = (((1,), (0,)), ((), ()))
NT = (((1,), (1,)), ((), ()))


def split(a):
    hi = a.astype(BF)
    return hi, (a - hi.astype(F32)).astype(BF)


def mm(a, b, dims):
    return lax.dot_general(a, b, dims, preferred_element_type=F32)


def dot3(a, b, dims):
    (ah, al), (bh, bl) = a, b
    rows = ah.shape[0]
    both = mm(jnp.concatenate([ah, al], 0), bh, dims)
    return both[:rows] + (both[rows:] + mm(ah, bl, dims))


def lanes(parts):
    return jnp.concatenate(parts, 1)


def prep_kernel(offs_hbm, d_hbm, l_hbm, r_hbm, mc, mch, c_out, zloc, fh, fl, bh, bl, dh, dl, offs, d_ref, l_ref, r_ref, sems, other):
    nb = d_ref.shape[0]
    width = r_ref.shape[0]
    rows = TAIL + width
    copies = [(pltpu.make_async_copy(offs_hbm, offs, other.at[0]), pltpu.make_async_copy(r_hbm, r_ref, other.at[1]))]
    for i in range(nb):
        copies.append(
            (
                pltpu.make_async_copy(d_hbm.at[i], d_ref.at[i], sems.at[0, i]),
                pltpu.make_async_copy(l_hbm.at[i], l_ref.at[i], sems.at[1, i]),
            )
        )
    for pair in copies:
        for copy in pair:
            copy.start()
    half = lax.rem(lax.axis_index("col"), 2)
    row = lax.broadcasted_iota(jnp.int32, (rows, BS), 0)
    lane = lax.broadcasted_iota(jnp.int32, (rows, BS), 1)
    for j in range(BW):
        fh[j] = jnp.where(row == lane + j * BS, 1.0, 0.0).astype(BF)
        fl[j] = jnp.zeros((rows, BS), BF)
    for copy in copies[0]:
        copy.wait()

    def block(i):
        for copy in copies[1 + i]:
            copy.wait()
        ds = split(d_ref[i])
        bcat = split(dot3(ds, split(lanes([l_ref[i, 0], l_ref[i, 1]])), NN))
        bh[i], bl[i] = bcat
        dh[i], dl[i] = ds
        return bcat, dot3(split(r_ref[:, i * BS : (i + 1) * BS]), ds, NT)

    ahead = block(0)
    for i in range(nb):
        bcat, own = ahead
        if i + 1 < nb:
            ahead = block(i + 1)
        p1 = BW + i - offs[0, i]
        p2 = BW + i - offs[1, i]
        prev = (lanes([fh[p1], fh[p2]]), lanes([fl[p1], fl[p2]]))
        z = -dot3(prev, bcat, NT)
        z = jnp.concatenate([z[:TAIL], z[TAIL:] + own], 0)
        zloc[i] = z[TAIL:]
        zh, zl = split(z)
        fh[BW + i] = zh
        fl[BW + i] = zl
        if i >= nb - BW:
            k = i - (nb - BW)
            mc[:, k * BS : (k + 1) * BS] = z
    hr = TAIL // 2
    start = pl.multiple_of(half * hr, hr)
    mch[:hr] = mc[pl.ds(start, hr), :]
    mch[hr:] = mc[TAIL:, :]
    c_out[...] = mc[TAIL:, :]


def energy_kernel(fh, fl, nd, ndh):
    nb = fh.shape[0] - BW
    hr = TAIL // 2
    half = lax.rem(lax.axis_index("col"), 2)
    start = pl.multiple_of(half * hr, hr)
    ah = lanes([fh[BW + i] for i in range(nb)])
    al = lanes([fl[BW + i] for i in range(nb)])
    full = dot3((ah, al), (ah[:TAIL], al[:TAIL]), NT)
    nd[:TAIL] = full[:TAIL]
    nd[TAIL:] = -full[TAIL:]
    ndh[:hr] = nd[pl.ds(start, hr), :]
    ndh[hr:] = nd[TAIL:, :]


def early_kernel(c_got, mc, t_out):
    t_out[...] = mc[TAIL:] + dot3(split(c_got[...]), split(mc[:TAIL]), NN)


def assemble(own, near, other, high, low, vec):
    parity = lax.rem(lax.axis_index("slab"), 2)
    half = lax.rem(lax.axis_index("col"), 2)
    hr = TAIL // 2
    mine, theirs = parity, 1 - parity
    h, l = split(own[:TAIL])
    high[mine], low[mine] = h, l
    vec[mine] = own[TAIL:]
    vec[theirs] = near[hr:]
    for ref, which in ((near, half), (other, 1 - half)):
        h, l = split(ref[:hr])
        at = pl.ds(pl.multiple_of(which * hr, hr), hr)
        high[theirs, at, :] = h
        low[theirs, at, :] = l


def step_rows(x, high, low, slot, dims):
    return dot3(split(x), (high[slot], low[slot]), dims)


def first_kernel(got_a, got_b, own, near, other, high, low, vec, t_out):
    assemble(own, near, other, high, low, vec)
    mid = vec[0] + step_rows(got_a[...] + got_b[...], high, low, 0, NN)
    t_out[...] = vec[1] + step_rows(mid, high, low, 1, NN)


def total(refs):
    out = refs[0][...]
    for ref in refs[1:]:
        out = out + ref[...]
    return out


def forward_kernel(n, *refs):
    got, (high, low, vec, t_out) = refs[:n], refs[n:]
    mid = vec[0] + step_rows(total(got), high, low, 0, NN)
    t_out[...] = vec[1] + step_rows(mid, high, low, 1, NN)


def turn_kernel(n, *refs):
    got, (mh, ml, c, nh, nl, d, e, u_out) = refs[:n], refs[n:]
    t_in = total(got)
    t_mid = c[0] + step_rows(t_in, mh, ml, 0, NN)
    e_odd = d[1] - step_rows(t_mid, nh, nl, 1, NN)
    e_even = d[0] - step_rows(t_in, nh, nl, 0, NN)
    e[0] = e_even
    e[1] = e_odd
    u_out[...] = step_rows(e_odd, mh, ml, 0, NT) + e_even


def inner_kernel(n, *refs):
    got, (mh, ml, c, fh, fl, zloc, z_out) = refs[:n], refs[n:]
    t_in = total(got)
    t_mid = c[0] + step_rows(t_in, mh, ml, 0, NN)
    odd = lax.rem(lax.axis_index("slab"), 2) == 1
    ts = split(jnp.where(odd, t_mid, t_in))
    for i in range(zloc.shape[0]):
        z_out[i] = zloc[i] + dot3(ts, (fh[BW + i, :TAIL], fl[BW + i, :TAIL]), NN)


def backward_kernel(n, *refs):
    got, (high, low, e, u_out) = refs[:n], refs[n:]
    mid = e[1] + step_rows(total(got), high, low, 1, NT)
    u_out[...] = step_rows(mid, high, low, 0, NT) + e[0]


def upward_kernel(offs, z, dh, dl, bh, bl, kh, kl, v, q):
    nb, width = z.shape[:2]
    row = lax.broadcasted_iota(jnp.int32, (TAIL, BS), 0)
    lane = lax.broadcasted_iota(jnp.int32, (TAIL, BS), 1)
    for i in range(nb + BW):
        q[i, :TAIL] = jnp.zeros((TAIL, BS), F32)
        if i >= nb:
            q[i, :TAIL] = jnp.where(row == lane + (i - nb) * BS, -1.0, 0.0)
        q[i, TAIL:] = z[i - BW] if i >= BW else jnp.zeros((width, BS), F32)
    for i in range(nb - 1, -1, -1):
        qs = split(q[BW + i])
        both = dot3(qs, (bh[i], bl[i]), NN)
        for k in range(2):
            at = BW + i - offs[k, i]
            q[at] = q[at] - both[:, k * BS : (k + 1) * BS]
        solved = dot3(qs, (dh[i], dl[i]), NN)
        cols = slice(i * BS, (i + 1) * BS)
        v[:, cols] = solved[TAIL:]
        kh[:, cols], kl[:, cols] = split(solved[:TAIL])


def solve_kernel(n, offs, *refs):
    got, (high, low, e, v, kh, kl, oh, ol, x, belowx, w, inner, tail, below, push) = refs[:n], refs[n:]
    width, size = v.shape
    odd = lax.rem(lax.axis_index("slab"), 2) == 1
    u_in = total(got)
    u_mid = e[1] + step_rows(u_in, high, low, 1, NT)
    u = jnp.where(odd, u_in, u_mid)
    solved = v[...] + dot3(split(u), (kh[...], kl[...]), NN)
    w[...] = solved
    inner[...] = solved
    tail[:width] = x[:, size - TAIL :]
    tail[width:] = solved[:, size - TAIL :]
    front = [solved[:, i * BS : (i + 1) * BS] for i in range(BW)]
    push_head(offs, front, oh, ol, push)
    below[:width] = belowx[...]
    for j in range(BW):
        below[width:, j * BS : (j + 1) * BS] = push[j]


def band_local(offs, s, ah, al, oh, ol, ext, acc, img, imt):
    nb = ah.shape[0]
    width = s.shape[0]
    for j in range(BW):
        ext[j] = jnp.zeros((width, BS), F32)
    for j in range(nb + BW):
        acc[j] = jnp.zeros((width, BS), F32)
    for i in range(nb):
        ext[BW + i] = s[:, i * BS : (i + 1) * BS]
    for i in range(nb):
        ss = split(ext[BW + i])
        os = (oh[i], ol[i])
        p1 = BW + i - offs[0, i]
        p2 = BW + i - offs[1, i]
        pulled = dot3(split(lanes([ext[p1], ext[p2]])), os, NT)
        both = dot3(ss, os, NN)
        acc[BW + i] = acc[BW + i] + pulled
        acc[p1] = acc[p1] + both[:, :BS]
        acc[p2] = acc[p2] + both[:, BS:]
    for i in range(nb):
        ss = split(ext[BW + i])
        ds = (ah[i], al[i])
        cols = slice(i * BS, (i + 1) * BS)
        img[:, cols] = acc[BW + i] + dot3(ss, ds, NT)
        imt[:, cols] = acc[BW + i] + dot3(ss, ds, NN)


def band_x_kernel(offs, s, a_hbm, o_hbm, img, imt, below, ah, al, oh, ol, ext, acc, a_ref, o_ref, sems):
    copies = (
        pltpu.make_async_copy(o_hbm, o_ref, sems.at[0]),
        pltpu.make_async_copy(a_hbm, a_ref, sems.at[1]),
    )
    for copy in copies:
        copy.start()
    for copy in copies:
        copy.wait()
    for i in range(ah.shape[0]):
        oh[i], ol[i] = split(lanes([o_ref[i, 0], o_ref[i, 1]]))
        ah[i], al[i] = split(a_ref[i])
    band_local(offs, s, ah, al, oh, ol, ext, acc, img, imt)
    for j in range(BW):
        below[:, j * BS : (j + 1) * BS] = acc[j]


def band_w_kernel(offs, s, ah, al, oh, ol, img, imt, ext, acc):
    band_local(offs, s, ah, al, oh, ol, ext, acc, img, imt)


def push_head(offs, s, oh, ol, push):
    for j in range(2 * BW):
        push[j] = jnp.zeros(push.shape[1:], F32)
    for i in range(BW):
        both = dot3(split(s[i]), (oh[i], ol[i]), NN)
        for k in range(2):
            at = BW + i - offs[k, i]
            push[at] = push[at] + both[:, k * BS : (k + 1) * BS]


def gram_kernel(count, nodes, offs, *refs):
    xs, ws = refs[:count], refs[count : 2 * count]
    (imgx, imtx, imgw, imtw, head, above, oh, ol, image, gram, left, right, hb) = refs[2 * count :]
    width = xs[0].shape[0]
    size = xs[0].shape[1]
    me = lax.axis_index("col")
    for j in range(BW):
        hb[j] = head[:, j * BS : (j + 1) * BS]
        hb[BW + j] = jnp.zeros((2 * width, BS), F32)
    for p, (img, imt) in enumerate(((imgx, imtx), (imgw, imtw))):
        rows = slice(p * width, (p + 1) * width)
        image[p] = img[...]
        image[p, :, size - TAIL :] = img[:, size - TAIL :] + above[rows]
        left[(2 + p) * width : (3 + p) * width] = imt[...]
        left[(2 + p) * width : (3 + p) * width, size - TAIL :] = imt[:, size - TAIL :] + above[rows]
        own = (xs, ws)[p][0]
        left[rows] = own[...]
        for k in range(count):
            at = jnp.bitwise_xor(me, k)
            right[pl.ds(pl.multiple_of((p * count + at) * width, width), width), :] = (xs, ws)[p][k][...]
    for i in range(BW):
        p1 = BW + i - offs[0, i]
        p2 = BW + i - offs[1, i]
        pulled = dot3(split(lanes([hb[p1], hb[p2]])), (oh[i], ol[i]), NT)
        cols = slice(i * BS, (i + 1) * BS)
        for p in range(2):
            part = pulled[p * width : (p + 1) * width]
            rows = slice((2 + p) * width, (3 + p) * width)
            image[p, :, cols] = image[p, :, cols] + part
            left[rows, cols] = left[rows, cols] + part
    gram[...] = dot3(split(left[...]), split(right[...]), NT) / nodes


def sum_kernel(*refs):
    parts, out = refs[:-1], refs[-1]
    whole = total(parts)
    width, half = out.shape[2], out.shape[4]
    for g in range(2):
        for p in range(2):
            at = (2 * g + p) * width
            for q in range(2):
                out[g, p, :, q, :] = whole[at : at + width, q * half : (q + 1) * half]


def call(kernel, outs, ins, smem=0, anys=0, last=0, scratch=(), flops=10**7):
    specs = [pl.BlockSpec(memory_space=pltpu.HBM)] * anys
    specs += [pl.BlockSpec(memory_space=pltpu.SMEM)] * smem
    specs += [pl.BlockSpec(memory_space=pltpu.VMEM)] * (len(ins) - smem - anys - last)
    specs += [pl.BlockSpec(memory_space=pltpu.HBM)] * last
    shapes = [jax.ShapeDtypeStruct(s, t) for s, t in outs]
    size = sum(a.size * a.dtype.itemsize for a in ins)
    return pl.pallas_call(
        kernel,
        out_shape=shapes,
        in_specs=specs,
        out_specs=[pl.BlockSpec(memory_space=pltpu.VMEM)] * len(shapes),
        scratch_shapes=scratch,
        cost_estimate=pl.CostEstimate(flops=flops, bytes_accessed=size, transcendentals=0),
        compiler_params=pltpu.CompilerParams(vmem_limit_bytes=32 * 2**20),
    )(*ins)


def gathered(value, axis):
    count = lax.axis_size(axis)
    parts = {0: value}
    step = count // 2
    while step:
        for k in list(parts):
            links = [(i, i ^ step) for i in range(count)]
            parts[k ^ step] = lax.ppermute(parts[k], axis, links)
        step //= 2
    return [parts[k] for k in range(count)]


def local_program(
    vectors, residual_block, diag_inverse, factor_blocks, band_diag, band_off, band_offsets
):
    width, size = vectors.shape
    nb = size // BS
    offsets = band_offsets.T
    slabs = lax.axis_size("slab")
    cols = lax.axis_size("col")
    pairs = slabs // 2
    rows = TAIL + width
    hrows = TAIL // 2 + width
    near = [(i, i ^ 1) for i in range(slabs)]
    cores = [(i, i ^ 1) for i in range(cols)]
    vec = ((width, TAIL), F32)
    flat = ((width, size), F32)
    matrix = [((2, TAIL, TAIL), BF)] * 2 + [((2, width, TAIL), F32)]

    mc, mch, c_own, zloc, fh, fl, bh, bl, dh, dl = call(
        prep_kernel,
        [((rows, TAIL), F32), ((hrows, TAIL), F32), vec, ((nb, width, BS), F32)]
        + [((nb + BW, rows, BS), BF)] * 2
        + [((nb, BS, 2 * BS), BF)] * 2
        + [((nb, BS, BS), BF)] * 2,
        [
            pltpu.with_memory_space_constraint(a, pltpu.HBM)
            for a in (offsets, diag_inverse, factor_blocks, residual_block)
        ],
        anys=4,
        scratch=[
            pltpu.SMEM(offsets.shape, jnp.int32),
            pltpu.VMEM(diag_inverse.shape, F32),
            pltpu.VMEM(factor_blocks.shape, F32),
            pltpu.VMEM(residual_block.shape, F32),
            pltpu.SemaphoreType.DMA((2, nb)),
            pltpu.SemaphoreType.DMA((2,)),
        ],
        flops=4 * 10**9,
    )
    c_got = lax.ppermute(c_own, "slab", [(0, 1)])
    m_near = lax.ppermute(mch, "slab", near)
    band_scratch = [pltpu.VMEM((nb + BW, width, BS), F32)] * 2
    imgx, imtx, belowx, ah, al, oh, ol = call(
        band_x_kernel,
        [flat, flat, vec] + [((nb, BS, BS), BF)] * 2 + [((nb, BS, 2 * BS), BF)] * 2,
        [offsets, vectors]
        + [pltpu.with_memory_space_constraint(a, pltpu.HBM) for a in (band_diag, band_off)],
        smem=1,
        last=2,
        scratch=band_scratch
        + [
            pltpu.VMEM(band_diag.shape, F32),
            pltpu.VMEM(band_off.shape, F32),
            pltpu.SemaphoreType.DMA((2,)),
        ],
        flops=10**9,
    )
    (t_out,) = call(early_kernel, [vec], [c_got, mc], flops=10**8)
    got_a = lax.ppermute(t_out, "slab", [(1, 3)])
    got_b = lax.ppermute(t_out, "slab", [(1, 2)])
    nd, ndh = call(
        energy_kernel, [((rows, TAIL), F32), ((hrows, TAIL), F32)], [fh, fl], flops=10**9
    )
    n_near = lax.ppermute(ndh, "slab", near)
    x_all = gathered(vectors, "col")
    up = [(i, i + 1) for i in range(slabs - 1)]
    down = [(i + 1, i) for i in range(slabs - 1)]
    m_other = lax.ppermute(m_near, "col", cores)
    n_other = lax.ppermute(n_near, "col", cores)

    mh, ml, c, t_out = call(
        first_kernel, matrix + [vec], [got_a, got_b, mc, m_near, m_other], flops=10**8
    )
    nh, nl, d = call(assemble, matrix, [nd, n_near, n_other], flops=10**8)
    got = [got_a, got_b]
    for h in range(2, pairs):
        hop = [(2 * h - 2, 2 * h), (2 * h - 1, 2 * h + 1)]
        got.append(lax.ppermute(t_out, "slab", hop))
        if h < pairs - 1:
            kernel = functools.partial(forward_kernel, len(got))
            (t_out,) = call(kernel, [vec], got + [mh, ml, c], flops=10**8)
    e, u_out = call(
        functools.partial(turn_kernel, len(got)),
        [((2, width, TAIL), F32), vec],
        got + [mh, ml, c, nh, nl, d],
        flops=10**8,
    )
    (z,) = call(
        functools.partial(inner_kernel, len(got)),
        [((nb, width, BS), F32)],
        got + [mh, ml, c, fh, fl, zloc],
        flops=2 * 10**8,
    )
    got = []
    for h in range(pairs - 1, 0, -1):
        hop = [(2 * h, 2 * h - 2), (2 * h + 1, 2 * h - 1)]
        got.append(lax.ppermute(u_out, "slab", hop))
        if h > 1:
            kernel = functools.partial(backward_kernel, len(got))
            (u_out,) = call(kernel, [vec], got + [mh, ml, e], flops=10**8)
    n_got = len(got)

    def last_kernel(offs, *refs):
        solve_kernel(n_got, offs, *refs)

    kh, kl, v = call(
        upward_kernel,
        [((TAIL, size), BF)] * 2 + [flat],
        [offsets, z, dh, dl, bh, bl],
        smem=1,
        scratch=[pltpu.VMEM((nb + BW, rows, BS), F32)],
        flops=4 * 10**9,
    )
    halo = ((2 * width, TAIL), F32)
    w, inner, tail, below = call(
        last_kernel,
        [flat, flat, halo, halo],
        [offsets] + got + [mh, ml, e, v, kh, kl, oh, ol, vectors, belowx],
        smem=1,
        scratch=[pltpu.VMEM((2 * BW, width, BS), F32)],
        flops=4 * 10**8,
    )
    w_all = gathered(inner, "col")
    head = lax.ppermute(tail, "slab", up)
    above = lax.ppermute(below, "slab", down)
    imgw, imtw = call(
        band_w_kernel,
        [flat, flat],
        [offsets, inner, ah, al, oh, ol],
        smem=1,
        scratch=band_scratch,
        flops=10**9,
    )
    image, gram = call(
        functools.partial(gram_kernel, cols, float(size * slabs)),
        [((2, width, size), F32), ((4 * width, 2 * cols * width), F32)],
        [offsets]
        + x_all
        + w_all
        + [imgx, imtx, imgw, imtw, head, above, oh, ol],
        smem=1,
        scratch=[
            pltpu.VMEM((4 * width, size), F32),
            pltpu.VMEM((2 * cols * width, size), F32),
            pltpu.VMEM((2 * BW, 2 * width, BS), F32),
        ],
        flops=10**9,
    )
    step = 1
    while step < slabs // 4:
        links = [(i, i ^ step) for i in range(slabs)]
        gram = gram + lax.ppermute(gram, "slab", links)
        step *= 2
    parts = [gram]
    for far in (step, 2 * step, 3 * step):
        parts.append(lax.ppermute(gram, "slab", [(i, i ^ far) for i in range(slabs)]))
    (gram,) = call(sum_kernel, [((2, 2, width, 2, cols * width), F32)], parts, flops=10**6)
    return (w, image, gram)


def solution(mesh):
    in_specs = (
        P("col", "slab"),
        P("col", "slab"),
        P("slab", None, None),
        P("slab", None, None, None),
        P("slab", None, None),
        P("slab", None, None, None),
        P("slab", None),
    )
    out_specs = (P("col", "slab"), P(None, "col", "slab"), P(None, None, "col", None, None))
    return jax.shard_map(
        local_program, mesh=mesh, in_specs=in_specs, out_specs=out_specs, check_vma=False
    )
```

profile of v0, /device:TPU:0, one launch (start us, length us, event | category | flops | bytes accessed | tf_op | source)
XLA Modules:
  0.0 89.1 jit_solution(12359508377262204468)
XLA Ops:
  0.6 6.6 %shard_map.94 = (f32[400,384]{1,0:T(8,128)S(1)}, f32[208,384]{1,0:T(8,128)S(1)}, f32[16,384]{1,0:T(8,128)S(1)}, f32[8,16,128]{2,1,0:T(8,128)S(1)}, bf16[11,400,1...) custom-call(s32[2,8]{1,0:T(2,128)} %bitcast.1, ...), custom_call_target="tpu_custom_call" | custom-call | flops 4000000000 | bytes 1638464 | tf_op jit(solution)/shard_map/pallas_call | solution.py:330
  7.2 3.1 %collective-permute-start.3 = (f32[208,384]{1,0:T(8,128)S(1)}, f32[208,384]{1,0:T(8,128)S(1)}, u32[]{:S(2)}, u32[]{:S(2)}) collective-permute-start(f32[208,384]{1,0:T(8,128)S(1)} %get-tuple-element.44), channel_id=1, source_target_pairs={{0,4},{4,0},{8,12},{12,8},{16,20},{20,16},{24,28},{28,24},{1,5},{5... | collective-permute-start | bytes 958472 | tf_op jit(solution)/shard_map/ppermute | solution.py:392
  10.3 1.5 %shard_map.98 = (f32[400,384]{1,0:T(8,128)S(1)}, f32[208,384]{1,0:T(8,128)S(1)}) custom-call(bf16[11,400,128]{2,1,0:T(8,128)(2,1)S(1)} %get-tuple-element.49.fh.refs_7_, bf16[11,400,128]{2,1,0:T(8,128)(2,1)S(1)} %get-tuple-element.50.fl.refs_8_), custom_call_target="tpu_custom_call" | custom-call | flops 1000000000 | bytes 2252800 | tf_op jit(solution)/shard_map/pallas_call | solution.py:330
  11.9 6.8 %collective-permute-done.3.near = f32[208,384]{1,0:T(8,128)S(1)} collective-permute-done((f32[208,384]{1,0:T(8,128)S(1)}, f32[208,384]{1,0:T(8,128)S(1)}, u32[]{:S(2)}, u32[]{:S(2)}) %collective-permute-start.3) | collective-permute-done | bytes 319520 | tf_op jit(solution)/shard_map/ppermute | solution.py:392
  18.7 6.0 %collective-permute-done.7.near = f32[208,384]{1,0:T(8,128)S(1)} collective-permute-done((f32[208,384]{1,0:T(8,128)S(1)}, f32[208,384]{1,0:T(8,128)S(1)}, u32[]{:S(2)}, u32[]{:S(2)}) %collective-permute-start.7) | collective-permute-done | bytes 319520 | tf_op jit(solution)/shard_map/ppermute | solution.py:415
  24.7 3.6 %collective-permute-start = (f32[16,384]{1,0:T(8,128)S(1)}, f32[16,384]{1,0:T(8,128)S(1)}, u32[]{:S(2)}, u32[]{:S(2)}) collective-permute-start(f32[16,384]{1,0:T(8,128)S(1)} %get-tuple-element.42), channel_id=1, source_target_pairs={{0,4},{1,5},{2,6},{3,7}} | collective-permute-start | bytes 73736 | tf_op jit(solution)/shard_map/ppermute | solution.py:391
  28.3 1.5 %collective-permute-done.c_got = f32[16,384]{1,0:T(8,128)S(1)} collective-permute-done((f32[16,384]{1,0:T(8,128)S(1)}, f32[16,384]{1,0:T(8,128)S(1)}, u32[]{:S(2)}, u32[]{:S(2)}) %collective-permute-start) | collective-permute-done | bytes 24608 | tf_op jit(solution)/shard_map/ppermute | solution.py:391
  30.0 0.7 collective-permute-start.1
  31.4 0.7 shard_map.96
  33.2 0.7 collective-permute-start.6
  34.1 0.7 shard_map.100
  34.8 0.8 collective-permute-start.9
  35.6 1.6 %collective-permute-start.13 = (f32[16,1024]{1,0:T(8,128)S(1)}, f32[16,1024]{1,0:T(8,128)S(1)}, u32[]{:S(2)}, u32[]{:S(2)}) collective-permute-start(f32[16,1024]{1,0:T(8,128)S(1)} %copy-done), channel_id=1, source_target_pairs={{0,2},{1,3},{2,0},{3,1},{4,6},{5,7},{6,4},{7,5},{8,10},{9,11},{10,... | collective-permute-start | bytes 196616 | tf_op jit(solution)/shard_map/ppermute | solution.py:348
  37.8 0.7 collective-permute-start.10
  38.5 2.9 %shard_map.105 = (f32[16,1024]{1,0:T(8,128)S(1)}, f32[16,1024]{1,0:T(8,128)S(1)}, f32[16,384]{1,0:T(8,128)S(1)}, bf16[8,128,128]{2,1,0:T(8,128)(2,1)S(1)}, bf16[...) custom-call(s32[2,8]{1,0:T(2,128)S(1)} %bitcast.2, ...), custom_call_target="tpu_custom_call" | custom-call | flops 1000000000 | bytes 1638464 | tf_op jit(solution)/shard_map/pallas_call | solution.py:330
  42.6 1.3 %collective-permute-start.11 = (f32[16,384]{1,0:T(8,128)S(1)}, f32[16,384]{1,0:T(8,128)S(1)}, u32[]{:S(2)}, u32[]{:S(2)}) collective-permute-start(f32[16,384]{1,0:T(8,128)S(1)} %shard_map.102), channel_id=1, source_target_pairs={{8,0},{12,4},{9,1},{13,5},{10,2},{14,6},{11,3},{15,7}} | collective-permute-start | bytes 73736 | tf_op jit(solution)/shard_map/ppermute | solution.py:448
  43.9 4.4 %shard_map.104 = (bf16[384,1024]{1,0:T(8,128)(2,1)S(1)}, bf16[384,1024]{1,0:T(8,128)(2,1)S(1)}, f32[16,1024]{1,0:T(8,128)S(1)}) custom-call(s32[2,8]{1,0:T(2,128)S(1)} %bitcast.3, f32[8,16,128]{2,1,0:T(8,128)S(1)} %shard_map.103.z, bf16[8,128,128]{2,1,0:T(8,128)(2,1)S(1)} %get-tuple-element.59.dh, bf16[8,128,128]{2,1,0:T(8,128)(2,1)S(1)} %get-tuple-element.60.dl, ...), custom_call_target="tpu_custom_call" | custom-call | flops 4000000000 | bytes 1638464 | tf_op jit(solution)/shard_map/pallas_call | solution.py:330
  48.3 12.8 %collective-permute-done.11.refs_2_ = f32[16,384]{1,0:T(8,128)S(1)} collective-permute-done((f32[16,384]{1,0:T(8,128)S(1)}, f32[16,384]{1,0:T(8,128)S(1)}, u32[]{:S(2)}, u32[]{:S(2)}) %collective-permute-start.11) | collective-permute-done | bytes 24608 | tf_op jit(solution)/shard_map/ppermute | solution.py:448
  61.1 1.9 %shard_map.106 = (f32[16,1024]{1,0:T(8,128)}, f32[16,1024]{1,0:T(8,128)S(1)}, f32[32,384]{1,0:T(8,128)S(1)}, f32[32,384]{1,0:T(8,128)S(1)}) custom-call(s32[2,8]{1,0:T(2,128)S(1)} %bitcast.4, f32[16,384]{1,0:T(8,128)S(1)} %collective-permute-done.9.refs_0_, f32[16,384]{1,0:T(8,128)S(1)} %collective-permute-done.10.refs_1_, ...), custom_call_target="tpu_custom_call" | custom-call | flops 400000000 | bytes 4079680 | tf_op jit(solution)/shard_map/pallas_call | solution.py:330
  62.9 1.5 %collective-permute-start.16 = (f32[16,1024]{1,0:T(8,128)S(1)}, f32[16,1024]{1,0:T(8,128)S(1)}, u32[]{:S(2)}, u32[]{:S(2)}) collective-permute-start(f32[16,1024]{1,0:T(8,128)S(1)} %get-tuple-element.70.s.refs_4_), channel_id=1, source_target_pairs={{0,2},{1,3},{2,0},{3,1},{4,6},{5,7},{6,4},{7,5},{8,10},{9,11},{10,... | collective-permute-start | bytes 196616 | tf_op jit(solution)/shard_map/ppermute | solution.py:348
  64.9 1.4 %collective-permute-start.18 = (f32[32,384]{1,0:T(8,128)S(1)}, f32[32,384]{1,0:T(8,128)S(1)}, u32[]{:S(2)}, u32[]{:S(2)}) collective-permute-start(f32[32,384]{1,0:T(8,128)S(1)} %get-tuple-element.77), channel_id=1, source_target_pairs={{0,4},{4,8},{8,12},{12,16},{16,20},{20,24},{24,28},{1,5},{5,9},{9,... | collective-permute-start | bytes 147464 | tf_op jit(solution)/shard_map/ppermute | solution.py:475
  66.4 1.3 %collective-permute-start.19 = (f32[32,384]{1,0:T(8,128)S(1)}, f32[32,384]{1,0:T(8,128)S(1)}, u32[]{:S(2)}, u32[]{:S(2)}) collective-permute-start(f32[32,384]{1,0:T(8,128)S(1)} %get-tuple-element.78), channel_id=1, source_target_pairs={{4,0},{8,4},{12,8},{16,12},{20,16},{24,20},{28,24},{5,1},{9,5},{13... | collective-permute-start | bytes 147464 | tf_op jit(solution)/shard_map/ppermute | solution.py:476
  67.7 1.5 %shard_map.107 = (f32[16,1024]{1,0:T(8,128)S(1)}, f32[16,1024]{1,0:T(8,128)S(1)}) custom-call(s32[2,8]{1,0:T(2,128)S(1)} %bitcast.5, f32[16,1024]{1,0:T(8,128)S(1)} %get-tuple-element.70.s.refs_4_, bf16[8,128,128]{2,1,0:T(8,128)(2,1)S(1)} %get-tuple-element.73.ah, bf16[8,128,128]{2,1,0:T(8,128)(2,1)S(1)} %get-tuple-element.74.al, ...), custom_call_target="tpu_custom_call" | custom-call | flops 1000000000 | bytes 1638464 | tf_op jit(solution)/shard_map/pallas_call | solution.py:330
  69.3 5.7 %collective-permute-done.19.refs_13_ = f32[32,384]{1,0:T(8,128)S(1)} collective-permute-done((f32[32,384]{1,0:T(8,128)S(1)}, f32[32,384]{1,0:T(8,128)S(1)}, u32[]{:S(2)}, u32[]{:S(2)}) %collective-permute-start.19) | collective-permute-done | bytes 49184 | tf_op jit(solution)/shard_map/ppermute | solution.py:476
  74.9 1.7 %shard_map.108 = (f32[2,16,1024]{2,1,0:T(8,128)}, f32[64,128]{1,0:T(8,128)S(1)}) custom-call(s32[2,8]{1,0:T(2,128)S(1)} %bitcast.6, f32[16,1024]{1,0:T(8,128)S(1)} %copy-done, f32[16,1024]{1,0:T(8,128)S(1)} %collective-permute-done.12.refs_1_, f32[16,1024]{1,0:T(8,128)S(1)} %collective-permute-done.13.refs_2_, ...), custom_call_target="tpu_custom_call" | custom-call | flops 1000000000 | bytes 1933376 | tf_op jit(solution)/shard_map/pallas_call | solution.py:330
  76.7 2.9 %collective-permute-start.20 = (f32[64,128]{1,0:T(8,128)S(1)}, f32[64,128]{1,0:T(8,128)S(1)}, u32[]{:S(2)}, u32[]{:S(2)}) collective-permute-start(f32[64,128]{1,0:T(8,128)S(1)} %get-tuple-element.80), channel_id=1, source_target_pairs={{0,4},{4,0},{8,12},{12,8},{16,20},{20,16},{24,28},{28,24},{1,5},{5... | collective-permute-start | bytes 98312 | tf_op jit(solution)/shard_map/ppermute | solution.py:503
  79.6 1.9 %collective-permute-done.20 = f32[64,128]{1,0:T(8,128)S(1)} collective-permute-done((f32[64,128]{1,0:T(8,128)S(1)}, f32[64,128]{1,0:T(8,128)S(1)}, u32[]{:S(2)}, u32[]{:S(2)}) %collective-permute-start.20) | collective-permute-done | bytes 32800 | tf_op jit(solution)/shard_map/ppermute | solution.py:503
  81.5 1.1 %collective-permute-start.21 = (f32[64,128]{1,0:T(8,128)S(1)}, f32[64,128]{1,0:T(8,128)S(1)}, u32[]{:S(2)}, u32[]{:S(2)}) collective-permute-start(f32[64,128]{1,0:T(8,128)S(1)} %add.3.refs_0_), channel_id=1, source_target_pairs={{0,8},{4,12},{8,0},{12,4},{16,24},{20,28},{24,16},{28,20},{1,9},{5... | collective-permute-start | bytes 98312 | tf_op jit(solution)/shard_map/ppermute | solution.py:507
  82.6 3.2 %collective-permute-start.23 = (f32[64,128]{1,0:T(8,128)S(1)}, f32[64,128]{1,0:T(8,128)S(1)}, u32[]{:S(2)}, u32[]{:S(2)}) collective-permute-start(f32[64,128]{1,0:T(8,128)S(1)} %add.3.refs_0_), channel_id=1, source_target_pairs={{0,24},{4,28},{8,16},{12,20},{16,8},{20,12},{24,0},{28,4},{1,25},{... | collective-permute-start | bytes 98312 | tf_op jit(solution)/shard_map/ppermute | solution.py:507
  85.9 1.6 %collective-permute-done.22.refs_2_ = f32[64,128]{1,0:T(8,128)S(1)} collective-permute-done((f32[64,128]{1,0:T(8,128)S(1)}, f32[64,128]{1,0:T(8,128)S(1)}, u32[]{:S(2)}, u32[]{:S(2)}) %collective-permute-start.22) | collective-permute-done | bytes 32800 | tf_op jit(solution)/shard_map/ppermute | solution.py:507
  87.4 0.9 %collective-permute-done.23.refs_3_ = f32[64,128]{1,0:T(8,128)S(1)} collective-permute-done((f32[64,128]{1,0:T(8,128)S(1)}, f32[64,128]{1,0:T(8,128)S(1)}, u32[]{:S(2)}, u32[]{:S(2)}) %collective-permute-start.23) | collective-permute-done | bytes 32800 | tf_op jit(solution)/shard_map/ppermute | solution.py:507
  88.3 0.8 shard_map.109
  (37 shorter events, 4.6 us)
Async XLA Ops:
  7.2 11.4 %collective-permute-start.3 = (f32[208,384]{1,0:T(8,128)S(1)}, f32[208,384]{1,0:T(8,128)S(1)}, u32[]{:S(2)}, u32[]{:S(2)}) collective-permute-start(f32[208,384]{1,0:T(8,128)S(1)} %get-tuple-element.44), channel_id=1, source_target_pairs={{0,4},{4,0},{8,12},{12,8},{16,20},{20,16},{24,28},{28,24},{1,5},{5... | collective-permute-start | bytes 958472 | tf_op jit(solution)/shard_map/ppermute | solution.py:392
  11.8 12.9 %collective-permute-start.7 = (f32[208,384]{1,0:T(8,128)S(1)}, f32[208,384]{1,0:T(8,128)S(1)}, u32[]{:S(2)}, u32[]{:S(2)}) collective-permute-start(f32[208,384]{1,0:T(8,128)S(1)} %get-tuple-element.52), channel_id=1, source_target_pairs={{0,4},{4,0},{8,12},{12,8},{16,20},{20,16},{24,28},{28,24},{1,5},{5... | collective-permute-start | bytes 958472 | tf_op jit(solution)/shard_map/ppermute | solution.py:415
  18.7 12.7 %collective-permute-start.4 = (f32[208,384]{1,0:T(8,128)S(1)}, f32[208,384]{1,0:T(8,128)S(1)}, u32[]{:S(2)}, u32[]{:S(2)}) collective-permute-start(f32[208,384]{1,0:T(8,128)S(1)} %collective-permute-done.3.near), channel_id=1, source_target_pairs={{0,1},{1,0},{2,3},{3,2},{4,5},{5,4},{6,7},{7,6},{8,9},{9,8},{10,11... | collective-permute-start | bytes 958472 | tf_op jit(solution)/shard_map/ppermute | solution.py:419
  24.7 9.2 %collective-permute-start.8 = (f32[208,384]{1,0:T(8,128)S(1)}, f32[208,384]{1,0:T(8,128)S(1)}, u32[]{:S(2)}, u32[]{:S(2)}) collective-permute-start(f32[208,384]{1,0:T(8,128)S(1)} %collective-permute-done.7.near), channel_id=1, source_target_pairs={{0,1},{1,0},{2,3},{3,2},{4,5},{5,4},{6,7},{7,6},{8,9},{9,8},{10,11... | collective-permute-start | bytes 958472 | tf_op jit(solution)/shard_map/ppermute | solution.py:420
  24.7 5.1 %collective-permute-start = (f32[16,384]{1,0:T(8,128)S(1)}, f32[16,384]{1,0:T(8,128)S(1)}, u32[]{:S(2)}, u32[]{:S(2)}) collective-permute-start(f32[16,384]{1,0:T(8,128)S(1)} %get-tuple-element.42), channel_id=1, source_target_pairs={{0,4},{1,5},{2,6},{3,7}} | collective-permute-start | bytes 73736 | tf_op jit(solution)/shard_map/ppermute | solution.py:391
  30.0 1.4 %collective-permute-start.1 = (f32[16,384]{1,0:T(8,128)S(1)}, f32[16,384]{1,0:T(8,128)S(1)}, u32[]{:S(2)}, u32[]{:S(2)}) collective-permute-start(f32[16,384]{1,0:T(8,128)S(1)} %shard_map.95), channel_id=1, source_target_pairs={{4,12},{5,13},{6,14},{7,15}} | collective-permute-start | bytes 73736 | tf_op jit(solution)/shard_map/ppermute | solution.py:410
  30.7 0.7 collective-permute-start.2
  32.1 0.7 collective-permute-start.5
  33.2 0.9 %collective-permute-start.6 = (f32[16,384]{1,0:T(8,128)S(1)}, f32[16,384]{1,0:T(8,128)S(1)}, u32[]{:S(2)}, u32[]{:S(2)}) collective-permute-start(f32[16,384]{1,0:T(8,128)S(1)} %shard_map.97), channel_id=1, source_target_pairs={{16,24},{20,28},{17,25},{21,29},{18,26},{22,30},{19,27},{23,31}} | collective-permute-start | bytes 73736 | tf_op jit(solution)/shard_map/ppermute | solution.py:429
  34.1 1.5 %copy-start = (f32[16,1024]{1,0:T(8,128)S(1)}, f32[16,1024]{1,0:T(8,128)}, u32[]{:S(2)}) copy-start(f32[16,1024]{1,0:T(8,128)} %refs_0_.1) | copy-start | bytes 196612
  34.8 3.6 %copy-start.1 = (s32[8,2]{0,1:T(2,128)S(1)}, s32[8,2]{0,1:T(2,128)}, u32[]{:S(2)}) copy-start(s32[8,2]{0,1:T(2,128)} %param.13) | copy-start | bytes 196
  34.8 2.4 %collective-permute-start.9 = (f32[16,384]{1,0:T(8,128)S(1)}, f32[16,384]{1,0:T(8,128)S(1)}, u32[]{:S(2)}, u32[]{:S(2)}) collective-permute-start(f32[16,384]{1,0:T(8,128)S(1)} %get-tuple-element.56), channel_id=1, source_target_pairs={{24,16},{28,20},{25,17},{29,21},{26,18},{30,22},{27,19},{31,23}} | collective-permute-start | bytes 73736 | tf_op jit(solution)/shard_map/ppermute | solution.py:448
  35.6 28.8 %collective-permute-start.13 = (f32[16,1024]{1,0:T(8,128)S(1)}, f32[16,1024]{1,0:T(8,128)S(1)}, u32[]{:S(2)}, u32[]{:S(2)}) collective-permute-start(f32[16,1024]{1,0:T(8,128)S(1)} %copy-done), channel_id=1, source_target_pairs={{0,2},{1,3},{2,0},{3,1},{4,6},{5,7},{6,4},{7,5},{8,10},{9,11},{10,... | collective-permute-start | bytes 196616 | tf_op jit(solution)/shard_map/ppermute | solution.py:348
  37.2 29.2 %collective-permute-start.12 = (f32[16,1024]{1,0:T(8,128)S(1)}, f32[16,1024]{1,0:T(8,128)S(1)}, u32[]{:S(2)}, u32[]{:S(2)}) collective-permute-start(f32[16,1024]{1,0:T(8,128)S(1)} %copy-done), channel_id=1, source_target_pairs={{0,1},{1,0},{2,3},{3,2},{4,5},{5,4},{6,7},{7,6},{8,9},{9,8},{10,11... | collective-permute-start | bytes 196616 | tf_op jit(solution)/shard_map/ppermute | solution.py:348
  37.8 4.2 %collective-permute-start.10 = (f32[16,384]{1,0:T(8,128)S(1)}, f32[16,384]{1,0:T(8,128)S(1)}, u32[]{:S(2)}, u32[]{:S(2)}) collective-permute-start(f32[16,384]{1,0:T(8,128)S(1)} %shard_map.101), channel_id=1, source_target_pairs={{16,8},{20,12},{17,9},{21,13},{18,10},{22,14},{19,11},{23,15}} | collective-permute-start | bytes 73736 | tf_op jit(solution)/shard_map/ppermute | solution.py:448
  42.6 18.5 %collective-permute-start.11 = (f32[16,384]{1,0:T(8,128)S(1)}, f32[16,384]{1,0:T(8,128)S(1)}, u32[]{:S(2)}, u32[]{:S(2)}) collective-permute-start(f32[16,384]{1,0:T(8,128)S(1)} %shard_map.102), channel_id=1, source_target_pairs={{8,0},{12,4},{9,1},{13,5},{10,2},{14,6},{11,3},{15,7}} | collective-permute-start | bytes 73736 | tf_op jit(solution)/shard_map/ppermute | solution.py:448
  62.9 4.7 %collective-permute-start.16 = (f32[16,1024]{1,0:T(8,128)S(1)}, f32[16,1024]{1,0:T(8,128)S(1)}, u32[]{:S(2)}, u32[]{:S(2)}) collective-permute-start(f32[16,1024]{1,0:T(8,128)S(1)} %get-tuple-element.70.s.refs_4_), channel_id=1, source_target_pairs={{0,2},{1,3},{2,0},{3,1},{4,6},{5,7},{6,4},{7,5},{8,10},{9,11},{10,... | collective-permute-start | bytes 196616 | tf_op jit(solution)/shard_map/ppermute | solution.py:348
  64.4 4.8 %collective-permute-start.14 = (f32[16,1024]{1,0:T(8,128)S(1)}, f32[16,1024]{1,0:T(8,128)S(1)}, u32[]{:S(2)}, u32[]{:S(2)}) collective-permute-start(f32[16,1024]{1,0:T(8,128)S(1)} %collective-permute-done.13.refs_2_), channel_id=1, source_target_pairs={{0,1},{1,0},{2,3},{3,2},{4,5},{5,4},{6,7},{7,6},{8,9},{9,8},{10,11... | collective-permute-start | bytes 196616 | tf_op jit(solution)/shard_map/ppermute | solution.py:348
  64.4 10.5 %collective-permute-start.15 = (f32[16,1024]{1,0:T(8,128)S(1)}, f32[16,1024]{1,0:T(8,128)S(1)}, u32[]{:S(2)}, u32[]{:S(2)}) collective-permute-start(f32[16,1024]{1,0:T(8,128)S(1)} %get-tuple-element.70.s.refs_4_), channel_id=1, source_target_pairs={{0,1},{1,0},{2,3},{3,2},{4,5},{5,4},{6,7},{7,6},{8,9},{9,8},{10,11... | collective-permute-start | bytes 196616 | tf_op jit(solution)/shard_map/ppermute | solution.py:348
  64.9 4.3 %collective-permute-start.18 = (f32[32,384]{1,0:T(8,128)S(1)}, f32[32,384]{1,0:T(8,128)S(1)}, u32[]{:S(2)}, u32[]{:S(2)}) collective-permute-start(f32[32,384]{1,0:T(8,128)S(1)} %get-tuple-element.77), channel_id=1, source_target_pairs={{0,4},{4,8},{8,12},{12,16},{16,20},{20,24},{24,28},{1,5},{5,9},{9,... | collective-permute-start | bytes 147464 | tf_op jit(solution)/shard_map/ppermute | solution.py:475
  66.4 8.6 %collective-permute-start.19 = (f32[32,384]{1,0:T(8,128)S(1)}, f32[32,384]{1,0:T(8,128)S(1)}, u32[]{:S(2)}, u32[]{:S(2)}) collective-permute-start(f32[32,384]{1,0:T(8,128)S(1)} %get-tuple-element.78), channel_id=1, source_target_pairs={{4,0},{8,4},{12,8},{16,12},{20,16},{24,20},{28,24},{5,1},{9,5},{13... | collective-permute-start | bytes 147464 | tf_op jit(solution)/shard_map/ppermute | solution.py:476
  67.7 7.3 %collective-permute-start.17 = (f32[16,1024]{1,0:T(8,128)S(1)}, f32[16,1024]{1,0:T(8,128)S(1)}, u32[]{:S(2)}, u32[]{:S(2)}) collective-permute-start(f32[16,1024]{1,0:T(8,128)S(1)} %collective-permute-done.16.refs_6_), channel_id=1, source_target_pairs={{0,1},{1,0},{2,3},{3,2},{4,5},{5,4},{6,7},{7,6},{8,9},{9,8},{10,11... | collective-permute-start | bytes 196616 | tf_op jit(solution)/shard_map/ppermute | solution.py:348
  76.7 4.8 %collective-permute-start.20 = (f32[64,128]{1,0:T(8,128)S(1)}, f32[64,128]{1,0:T(8,128)S(1)}, u32[]{:S(2)}, u32[]{:S(2)}) collective-permute-start(f32[64,128]{1,0:T(8,128)S(1)} %get-tuple-element.80), channel_id=1, source_target_pairs={{0,4},{4,0},{8,12},{12,8},{16,20},{20,16},{24,28},{28,24},{1,5},{5... | collective-permute-start | bytes 98312 | tf_op jit(solution)/shard_map/ppermute | solution.py:503
  81.5 4.4 %collective-permute-start.21 = (f32[64,128]{1,0:T(8,128)S(1)}, f32[64,128]{1,0:T(8,128)S(1)}, u32[]{:S(2)}, u32[]{:S(2)}) collective-permute-start(f32[64,128]{1,0:T(8,128)S(1)} %add.3.refs_0_), channel_id=1, source_target_pairs={{0,8},{4,12},{8,0},{12,4},{16,24},{20,28},{24,16},{28,20},{1,9},{5... | collective-permute-start | bytes 98312 | tf_op jit(solution)/shard_map/ppermute | solution.py:507
  82.6 4.8 %collective-permute-start.22 = (f32[64,128]{1,0:T(8,128)S(1)}, f32[64,128]{1,0:T(8,128)S(1)}, u32[]{:S(2)}, u32[]{:S(2)}) collective-permute-start(f32[64,128]{1,0:T(8,128)S(1)} %add.3.refs_0_), channel_id=1, source_target_pairs={{0,16},{4,20},{8,24},{12,28},{16,0},{20,4},{24,8},{28,12},{1,17},{... | collective-permute-start | bytes 98312 | tf_op jit(solution)/shard_map/ppermute | solution.py:507
  82.6 5.7 %collective-permute-start.23 = (f32[64,128]{1,0:T(8,128)S(1)}, f32[64,128]{1,0:T(8,128)S(1)}, u32[]{:S(2)}, u32[]{:S(2)}) collective-permute-start(f32[64,128]{1,0:T(8,128)S(1)} %add.3.refs_0_), channel_id=1, source_target_pairs={{0,24},{4,28},{8,16},{12,20},{16,8},{20,12},{24,0},{28,4},{1,25},{... | collective-permute-start | bytes 98312 | tf_op jit(solution)/shard_map/ppermute | solution.py:507
where the time goes:
time: 89.4 us; the launch traced here: 89.1 us
  waiting for transfers between devices  37.2 us (42%)
  starting transfers between devices  25.8 us (29%)
  Pallas kernels  25.2 us (28%)
    pallas_call x16, Pallas kernels, call(): pl.pallas_call(kernel, out_shape=shapes, in_specs=specs, out_specs=[pl.Bl...  25.2 us
    ppermute x3, waiting for transfers between devices, local_program(): got.append(lax.ppermute(u_out, 'slab', hop))  12.8 us
    ppermute x1, waiting for transfers between devices, local_program(): m_near = lax.ppermute(mch, 'slab', near)  6.81 us
    ppermute x1, waiting for transfers between devices, local_program(): n_near = lax.ppermute(ndh, 'slab', near)  6.01 us
    ppermute x1, waiting for transfers between devices, local_program(): above = lax.ppermute(below, 'slab', down)  5.65 us
    ppermute x3, starting transfers between devices, local_program(): lax.ppermute(gram, 'slab', [(i, i ^ far) for i in range(slabs)])  4.39 us
    ppermute x1, starting transfers between devices, local_program(): c_got = lax.ppermute(c_own, 'slab', [(0, 1)])  3.63 us
    ppermute x6, starting transfers between devices, gathered(): parts[k ^ step] = lax.ppermute(parts[k], axis, links)  3.63 us
  transfers between devices with their start and end apart: 24, of which 8 were waited for; matrix products, arithmetic and copies ran while one was open for 0% of the time, Pallas kernels for 17%

commit v1 on v0

--- a/solution.py
+++ b/solution.py
@@ -28,7 +28,11 @@
 
 def dot3(a, b, dims):
     (ah, al), (bh, bl) = a, b
-    rows = ah.shape[0]
+    rows, depth = ah.shape
+    if depth <= BS:
+        axis = dims[0][1][0]
+        twice = mm(jnp.concatenate([ah, al], 1), jnp.concatenate([bh, bh], axis), dims)
+        return twice + mm(ah, bl, dims)
     both = mm(jnp.concatenate([ah, al], 0), bh, dims)
     return both[:rows] + (both[rows:] + mm(ah, bl, dims))
 
@@ -151,6 +155,23 @@
     t_out[...] = vec[1] + step_rows(mid, high, low, 1, NN)
 
 
+def compose_kernel(high, low, half_out):
+    hr = TAIL // 2
+    start = pl.multiple_of(lax.rem(lax.axis_index("col"), 2) * hr, hr)
+    mine = (high[0, pl.ds(start, hr), :], low[0, pl.ds(start, hr), :])
+    half_out[...] = dot3(mine, (high[1], low[1]), NN)
+
+
+def join_kernel(near, other, high, low):
+    half = lax.rem(lax.axis_index("col"), 2)
+    hr = TAIL // 2
+    for ref, which in ((near, half), (other, 1 - half)):
+        h, l = split(ref[...])
+        at = pl.ds(pl.multiple_of(which * hr, hr), hr)
+        high[at, :] = h
+        low[at, :] = l
+
+
 def turn_kernel(n, *refs):
     got, (mh, ml, c, nh, nl, d, e, u_out) = refs[:n], refs[n:]
     t_in = total(got)
@@ -178,7 +199,21 @@
     u_out[...] = step_rows(mid, high, low, 0, NT) + e[0]
 
 
-def upward_kernel(offs, z, dh, dl, bh, bl, kh, kl, v, q):
+def upward_steps(offs, dh, dl, bh, bl, q, kh, kl, v, blocks):
+    first = blocks[0]
+    for i in reversed(blocks):
+        qs = split(q[BW + i])
+        both = dot3(qs, (bh[i], bl[i]), NN)
+        for k in range(2):
+            at = BW + i - offs[k, i]
+            q[at] = q[at] - both[:, k * BS : (k + 1) * BS]
+        solved = dot3(qs, (dh[i], dl[i]), NN)
+        cols = slice((i - first) * BS, (i - first + 1) * BS)
+        v[:, cols] = solved[TAIL:]
+        kh[:, cols], kl[:, cols] = split(solved[:TAIL])
+
+
+def upward_kernel(offs, z, dh, dl, bh, bl, q, kh, kl, v):
     nb, width = z.shape[:2]
     row = lax.broadcasted_iota(jnp.int32, (TAIL, BS), 0)
     lane = lax.broadcasted_iota(jnp.int32, (TAIL, BS), 1)
@@ -187,26 +222,32 @@
         if i >= nb:
             q[i, :TAIL] = jnp.where(row == lane + (i - nb) * BS, -1.0, 0.0)
         q[i, TAIL:] = z[i - BW] if i >= BW else jnp.zeros((width, BS), F32)
-    for i in range(nb - 1, -1, -1):
-        qs = split(q[BW + i])
-        both = dot3(qs, (bh[i], bl[i]), NN)
-        for k in range(2):
-            at = BW + i - offs[k, i]
-            q[at] = q[at] - both[:, k * BS : (k + 1) * BS]
-        solved = dot3(qs, (dh[i], dl[i]), NN)
-        cols = slice(i * BS, (i + 1) * BS)
-        v[:, cols] = solved[TAIL:]
-        kh[:, cols], kl[:, cols] = split(solved[:TAIL])
+    upward_steps(offs, dh, dl, bh, bl, q, kh, kl, v, range(nb // 2, nb))
+
+
+def upward_rest_kernel(offs, q_in, dh, dl, bh, bl, kh, kl, v, q):
+    nb = dh.shape[0]
+    for i in range(nb // 2 + BW):
+        q[i] = q_in[i]
+    upward_steps(offs, dh, dl, bh, bl, q, kh, kl, v, range(nb // 2))
 
 
 def solve_kernel(n, offs, *refs):
-    got, (high, low, e, v, kh, kl, oh, ol, x, belowx, w, inner, tail, below, push) = refs[:n], refs[n:]
-    width, size = v.shape
+    got, rest = refs[:n], refs[n:]
+    (skip, ph, plow, high, low, e, va, kha, kla, vb, khb, klb, oh, ol, x, belowx) = rest[:16]
+    (w, inner, tail, below, push) = rest[16:]
+    width, size = x.shape
     odd = lax.rem(lax.axis_index("slab"), 2) == 1
-    u_in = total(got)
+    u_in = total(got) + dot3(split(skip[...]), (ph[...], plow[...]), NT)
     u_mid = e[1] + step_rows(u_in, high, low, 1, NT)
     u = jnp.where(odd, u_in, u_mid)
-    solved = v[...] + dot3(split(u), (kh[...], kl[...]), NN)
+    us = split(u)
+    solved = lanes(
+        [
+            vb[...] + dot3(us, (khb[...], klb[...]), NN),
+            va[...] + dot3(us, (kha[...], kla[...]), NN),
+        ]
+    )
     w[...] = solved
     inner[...] = solved
     tail[:width] = x[:, size - TAIL :]
@@ -422,6 +463,10 @@
     mh, ml, c, t_out = call(
         first_kernel, matrix + [vec], [got_a, got_b, mc, m_near, m_other], flops=10**8
     )
+    (composed,) = call(compose_kernel, [((TAIL // 2, TAIL), F32)], [mh, ml], flops=4 * 10**8)
+    q_near = lax.ppermute(composed, "slab", [(2, 0), (3, 1)])
+    q_other = lax.ppermute(q_near, "col", cores)
+    ph, plow = call(join_kernel, [((TAIL, TAIL), BF)] * 2, [q_near, q_other], flops=10**6)
     nh, nl, d = call(assemble, matrix, [nd, n_near, n_other], flops=10**8)
     got = [got_a, got_b]
     for h in range(2, pairs):
@@ -443,30 +488,50 @@
         flops=2 * 10**8,
     )
     got = []
-    for h in range(pairs - 1, 0, -1):
+    for h in range(pairs - 1, 1, -1):
+        if h == 2:
+            skip = lax.ppermute(u_out, "slab", [(4, 0), (5, 1)])
         hop = [(2 * h, 2 * h - 2), (2 * h + 1, 2 * h - 1)]
+        if h == pairs - 1:
+            e_out = u_out
+            if h > 2:
+                hop += [(2, 0), (3, 1)]
         got.append(lax.ppermute(u_out, "slab", hop))
-        if h > 1:
+        if h > 2:
             kernel = functools.partial(backward_kernel, len(got))
             (u_out,) = call(kernel, [vec], got + [mh, ml, e], flops=10**8)
+    if pairs == 3:
+        got.append(lax.ppermute(e_out, "slab", [(2, 0), (3, 1)]))
     n_got = len(got)
 
     def last_kernel(offs, *refs):
         solve_kernel(n_got, offs, *refs)
 
-    kh, kl, v = call(
+    half = nb // 2
+    factors = [dh, dl, bh, bl]
+    state = ((nb + BW, rows, BS), F32)
+    q, kha, kla, va = call(
         upward_kernel,
-        [((TAIL, size), BF)] * 2 + [flat],
-        [offsets, z, dh, dl, bh, bl],
+        [state] + [((TAIL, (nb - half) * BS), BF)] * 2 + [((width, (nb - half) * BS), F32)],
+        [offsets, z] + factors,
         smem=1,
-        scratch=[pltpu.VMEM((nb + BW, rows, BS), F32)],
-        flops=4 * 10**9,
+        flops=2 * 10**9,
+    )
+    khb, klb, vb = call(
+        upward_rest_kernel,
+        [((TAIL, half * BS), BF)] * 2 + [((width, half * BS), F32)],
+        [offsets, q] + factors,
+        smem=1,
+        scratch=[pltpu.VMEM(*state)],
+        flops=2 * 10**9,
     )
     halo = ((2 * width, TAIL), F32)
     w, inner, tail, below = call(
         last_kernel,
         [flat, flat, halo, halo],
-        [offsets] + got + [mh, ml, e, v, kh, kl, oh, ol, vectors, belowx],
+        [offsets]
+        + got
+        + [skip, ph, plow, mh, ml, e, va, kha, kla, vb, khb, klb, oh, ol, vectors, belowx],
         smem=1,
         scratch=[pltpu.VMEM((2 * BW, width, BS), F32)],
         flops=4 * 10**8,

time: 89.4 us -> 82.5 us (0.923)
  waiting for transfers between devices: 37.2 us -> 28.3 us
  starting transfers between devices: 25.8 us -> 28 us
    ppermute x3 -> x2, waiting for transfers between devices: 12.8 us -> 3.09 us  [local_program(): got.append(lax.ppermute(u_out, 'slab', hop))]
    ppermute x0 -> x3, waiting for transfers between devices: none -> 8.2 us  [the longest x1 5.11 us: local_program(): skip = lax.ppermute(u_out, 'slab', [(4, 0), (5, 1)])]
    ppermute x1, waiting for transfers between devices: 6.01 us -> 0.01 us  [local_program(): n_near = lax.ppermute(ndh, 'slab', near)]
    ppermute x1, waiting for transfers between devices: 5.65 us -> 3 us  [local_program(): above = lax.ppermute(below, 'slab', down)]
    ppermute x0 -> x3, starting transfers between devices: none -> 2.59 us  [the longest x1 1.29 us: local_program(): q_near = lax.ppermute(composed, 'slab', [(2, 0), (3, 1)])]
    ppermute x1, starting transfers between devices: 2.91 us -> 0.91 us  [local_program(): gram = gram + lax.ppermute(gram, 'slab', links)]
    ppermute x1, starting transfers between devices: 1.4 us -> 2.8 us  [local_program(): head = lax.ppermute(tail, 'slab', up)]
    ppermute x1, waiting for transfers between devices: 1.89 us -> 3 us  [local_program(): gram = gram + lax.ppermute(gram, 'slab', links)]
  transfers between devices with their start and end apart: 24 -> 26, of which waited for: 8 -> 9; matrix products, arithmetic and copies ran while one was open for 0% -> 0% of each run, Pallas kernels for 17% -> 20%
where the time goes in v1:
time: 82.5 us; the launch traced here: 82.2 us
  waiting for transfers between devices  28.3 us (34%)
  starting transfers between devices  28 us (34%)
  Pallas kernels  25 us (30%)
  between operations  0.94 us (1%)
    pallas_call x18, Pallas kernels, call(): pl.pallas_call(kernel, out_shape=shapes, in_specs=specs, out_specs=[pl.Bl...  25 us
    ppermute x1, waiting for transfers between devices, local_program(): m_near = lax.ppermute(mch, 'slab', near)  6.82 us
    ppermute x1, waiting for transfers between devices, local_program(): skip = lax.ppermute(u_out, 'slab', [(4, 0), (5, 1)])  5.11 us
    ppermute x3, starting transfers between devices, local_program(): lax.ppermute(gram, 'slab', [(i, i ^ far) for i in range(slabs)])  4.39 us
    ppermute x6, starting transfers between devices, gathered(): parts[k ^ step] = lax.ppermute(parts[k], axis, links)  4.1 us
    ppermute x1, starting transfers between devices, local_program(): c_got = lax.ppermute(c_own, 'slab', [(0, 1)])  3.91 us
    ppermute x2, waiting for transfers between devices, local_program(): got.append(lax.ppermute(u_out, 'slab', hop))  3.09 us
    ppermute x1, waiting for transfers between devices, local_program(): q_near = lax.ppermute(composed, 'slab', [(2, 0), (3, 1)])  3.08 us
  transfers between devices with their start and end apart: 26, of which 9 were waited for; matrix products, arithmetic and copies ran while one was open for 0% of the time, Pallas kernels for 20%

profile of v1, /device:TPU:0, one launch (start us, length us, event | category | flops | bytes accessed | tf_op | source)
XLA Modules:
  0.0 82.2 jit_solution(16781340835846928257)
XLA Ops:
  0.6 6.4 %shard_map.94 = (f32[400,384]{1,0:T(8,128)S(1)}, f32[208,384]{1,0:T(8,128)S(1)}, f32[16,384]{1,0:T(8,128)S(1)}, f32[8,16,128]{2,1,0:T(8,128)S(1)}, bf16[11,400,1...) custom-call(s32[2,8]{1,0:T(2,128)} %bitcast.1, ...), custom_call_target="tpu_custom_call" | custom-call | flops 4000000000 | bytes 1638464 | tf_op jit(solution)/shard_map/pallas_call | solution.py:371
  7.0 3.1 %collective-permute-start.3 = (f32[208,384]{1,0:T(8,128)S(1)}, f32[208,384]{1,0:T(8,128)S(1)}, u32[]{:S(2)}, u32[]{:S(2)}) collective-permute-start(f32[208,384]{1,0:T(8,128)S(1)} %get-tuple-element.50), channel_id=1, source_target_pairs={{0,4},{4,0},{8,12},{12,8},{16,20},{20,16},{24,28},{28,24},{1,5},{5... | collective-permute-start | bytes 958472 | tf_op jit(solution)/shard_map/ppermute | solution.py:433
  10.1 1.5 %shard_map.98 = (f32[400,384]{1,0:T(8,128)S(1)}, f32[208,384]{1,0:T(8,128)S(1)}) custom-call(bf16[11,400,128]{2,1,0:T(8,128)(2,1)S(1)} %get-tuple-element.55.fh.refs_7_, bf16[11,400,128]{2,1,0:T(8,128)(2,1)S(1)} %get-tuple-element.56.fl.refs_8_), custom_call_target="tpu_custom_call" | custom-call | flops 1000000000 | bytes 2252800 | tf_op jit(solution)/shard_map/pallas_call | solution.py:371
  11.7 6.8 %collective-permute-done.3.near = f32[208,384]{1,0:T(8,128)S(1)} collective-permute-done((f32[208,384]{1,0:T(8,128)S(1)}, f32[208,384]{1,0:T(8,128)S(1)}, u32[]{:S(2)}, u32[]{:S(2)}) %collective-permute-start.3) | collective-permute-done | bytes 319520 | tf_op jit(solution)/shard_map/ppermute | solution.py:433
  18.5 3.9 %collective-permute-start = (f32[16,384]{1,0:T(8,128)S(1)}, f32[16,384]{1,0:T(8,128)S(1)}, u32[]{:S(2)}, u32[]{:S(2)}) collective-permute-start(f32[16,384]{1,0:T(8,128)S(1)} %get-tuple-element.48), channel_id=1, source_target_pairs={{0,4},{1,5},{2,6},{3,7}} | collective-permute-start | bytes 73736 | tf_op jit(solution)/shard_map/ppermute | solution.py:432
  22.4 1.9 %collective-permute-done.c_got = f32[16,384]{1,0:T(8,128)S(1)} collective-permute-done((f32[16,384]{1,0:T(8,128)S(1)}, f32[16,384]{1,0:T(8,128)S(1)}, u32[]{:S(2)}, u32[]{:S(2)}) %collective-permute-start) | collective-permute-done | bytes 24608 | tf_op jit(solution)/shard_map/ppermute | solution.py:432
  24.5 0.8 collective-permute-start.1
  27.2 1.3 %collective-permute-start.12 = (f32[192,384]{1,0:T(8,128)S(1)}, f32[192,384]{1,0:T(8,128)S(1)}, u32[]{:S(2)}, u32[]{:S(2)}) collective-permute-start(f32[192,384]{1,0:T(8,128)S(1)} %shard_map.102), channel_id=1, source_target_pairs={{8,0},{12,4},{9,1},{13,5},{10,2},{14,6},{11,3},{15,7}} | collective-permute-start | bytes 884744 | tf_op jit(solution)/shard_map/ppermute | solution.py:467
  29.7 1.5 %collective-permute-start.15 = (f32[16,1024]{1,0:T(8,128)S(1)}, f32[16,1024]{1,0:T(8,128)S(1)}, u32[]{:S(2)}, u32[]{:S(2)}) collective-permute-start(f32[16,1024]{1,0:T(8,128)S(1)} %copy-done), channel_id=1, source_target_pairs={{0,2},{1,3},{2,0},{3,1},{4,6},{5,7},{6,4},{7,5},{8,10},{9,11},{10,... | collective-permute-start | bytes 196616 | tf_op jit(solution)/shard_map/ppermute | solution.py:389
  32.3 3.0 %shard_map.107 = (f32[16,1024]{1,0:T(8,128)S(1)}, f32[16,1024]{1,0:T(8,128)S(1)}, f32[16,384]{1,0:T(8,128)S(1)}, bf16[8,128,128]{2,1,0:T(8,128)(2,1)S(1)}, bf16[...) custom-call(s32[2,8]{1,0:T(2,128)S(1)} %bitcast.2, ...), custom_call_target="tpu_custom_call" | custom-call | flops 1000000000 | bytes 1638464 | tf_op jit(solution)/shard_map/pallas_call | solution.py:371
  35.5 0.7 shard_map.100
  36.2 1.3 %collective-permute-start.9 = (f32[16,384]{1,0:T(8,128)S(1)}, f32[16,384]{1,0:T(8,128)S(1)}, u32[]{:S(2)}, u32[]{:S(2)}) collective-permute-start(f32[16,384]{1,0:T(8,128)S(1)} %get-tuple-element.62), channel_id=1, source_target_pairs={{24,16},{28,20},{8,0},{12,4},{25,17},{29,21},{9,1},{13,5},{26,18},... | collective-permute-start | bytes 73736 | tf_op jit(solution)/shard_map/ppermute | solution.py:499
  38.1 3.1 %collective-permute-done.12.near = f32[192,384]{1,0:T(8,128)S(1)} collective-permute-done((f32[192,384]{1,0:T(8,128)S(1)}, f32[192,384]{1,0:T(8,128)S(1)}, u32[]{:S(2)}, u32[]{:S(2)}) %collective-permute-start.12) | collective-permute-done | bytes 294944 | tf_op jit(solution)/shard_map/ppermute | solution.py:467
  41.2 2.1 %shard_map.105 = (f32[11,400,128]{2,1,0:T(8,128)S(1)}, bf16[384,512]{1,0:T(8,128)(2,1)S(1)}, bf16[384,512]{1,0:T(8,128)(2,1)S(1)}, f32[16,512]{1,0:T(8,128)S(1)}) custom-call(s32[2,8]{1,0:T(2,128)S(1)} %bitcast.3, f32[8,16,128]{2,1,0:T(8,128)S(1)} %shard_map.104.z, bf16[8,128,128]{2,1,0:T(8,128)(2,1)S(1)} %get-tuple-element.67.dh, ...), custom_call_target="tpu_custom_call" | custom-call | flops 2000000000 | bytes 1638464 | tf_op jit(solution)/shard_map/pallas_call | solution.py:371
  43.3 3.1 %collective-permute-done.9.refs_0_ = f32[16,384]{1,0:T(8,128)S(1)} collective-permute-done((f32[16,384]{1,0:T(8,128)S(1)}, f32[16,384]{1,0:T(8,128)S(1)}, u32[]{:S(2)}, u32[]{:S(2)}) %collective-permute-start.9) | collective-permute-done | bytes 24608 | tf_op jit(solution)/shard_map/ppermute | solution.py:499
  47.0 0.7 collective-permute-start.10
  47.7 1.3 %collective-permute-start.11 = (f32[16,384]{1,0:T(8,128)S(1)}, f32[16,384]{1,0:T(8,128)S(1)}, u32[]{:S(2)}, u32[]{:S(2)}) collective-permute-start(f32[16,384]{1,0:T(8,128)S(1)} %shard_map.101), channel_id=1, source_target_pairs={{16,0},{20,4},{17,1},{21,5},{18,2},{22,6},{19,3},{23,7}} | collective-permute-start | bytes 73736 | tf_op jit(solution)/shard_map/ppermute | solution.py:493
  49.0 2.0 %shard_map.106 = (bf16[384,512]{1,0:T(8,128)(2,1)S(1)}, bf16[384,512]{1,0:T(8,128)(2,1)S(1)}, f32[16,512]{1,0:T(8,128)S(1)}) custom-call(s32[2,8]{1,0:T(2,128)S(1)} %bitcast.4, f32[11,400,128]{2,1,0:T(8,128)S(1)} %get-tuple-element.74.q_in, bf16[8,128,128]{2,1,0:T(8,128)(2,1)S(1)} %get-tuple-element.67.dh, bf16[8,128,128]{2,1,0:T(8,128)(2,1)S(1)} %get-tuple-element.68.dl, ...), custom_call_target="tpu_custom_call" | custom-call | flops 2000000000 | bytes 3825728 | tf_op jit(solution)/shard_map/pallas_call | solution.py:371
  51.1 5.1 %collective-permute-done.11.refs_2_ = f32[16,384]{1,0:T(8,128)S(1)} collective-permute-done((f32[16,384]{1,0:T(8,128)S(1)}, f32[16,384]{1,0:T(8,128)S(1)}, u32[]{:S(2)}, u32[]{:S(2)}) %collective-permute-start.11) | collective-permute-done | bytes 24608 | tf_op jit(solution)/shard_map/ppermute | solution.py:493
  56.2 2.0 %shard_map.108 = (f32[16,1024]{1,0:T(8,128)}, f32[16,1024]{1,0:T(8,128)S(1)}, f32[32,384]{1,0:T(8,128)S(1)}, f32[32,384]{1,0:T(8,128)S(1)}) custom-call(s32[2,8]{1,0:T(2,128)S(1)} %bitcast.5, f32[16,384]{1,0:T(8,128)S(1)} %collective-permute-done.9.refs_0_, f32[16,384]{1,0:T(8,128)S(1)} %collective-permute-done.10.refs_1_, ...), custom_call_target="tpu_custom_call" | custom-call | flops 400000000 | bytes 4669504 | tf_op jit(solution)/shard_map/pallas_call | solution.py:371
  58.3 1.5 %collective-permute-start.18 = (f32[16,1024]{1,0:T(8,128)S(1)}, f32[16,1024]{1,0:T(8,128)S(1)}, u32[]{:S(2)}, u32[]{:S(2)}) collective-permute-start(f32[16,1024]{1,0:T(8,128)S(1)} %get-tuple-element.82.s.refs_4_), channel_id=1, source_target_pairs={{0,2},{1,3},{2,0},{3,1},{4,6},{5,7},{6,4},{7,5},{8,10},{9,11},{10,... | collective-permute-start | bytes 196616 | tf_op jit(solution)/shard_map/ppermute | solution.py:389
  60.3 2.8 %collective-permute-start.20 = (f32[32,384]{1,0:T(8,128)S(1)}, f32[32,384]{1,0:T(8,128)S(1)}, u32[]{:S(2)}, u32[]{:S(2)}) collective-permute-start(f32[32,384]{1,0:T(8,128)S(1)} %get-tuple-element.89), channel_id=1, source_target_pairs={{0,4},{4,8},{8,12},{12,16},{16,20},{20,24},{24,28},{1,5},{5,9},{9,... | collective-permute-start | bytes 147464 | tf_op jit(solution)/shard_map/ppermute | solution.py:540
  63.1 1.3 %collective-permute-start.21 = (f32[32,384]{1,0:T(8,128)S(1)}, f32[32,384]{1,0:T(8,128)S(1)}, u32[]{:S(2)}, u32[]{:S(2)}) collective-permute-start(f32[32,384]{1,0:T(8,128)S(1)} %get-tuple-element.90), channel_id=1, source_target_pairs={{4,0},{8,4},{12,8},{16,12},{20,16},{24,20},{28,24},{5,1},{9,5},{13... | collective-permute-start | bytes 147464 | tf_op jit(solution)/shard_map/ppermute | solution.py:541
  64.5 1.6 %shard_map.109 = (f32[16,1024]{1,0:T(8,128)S(1)}, f32[16,1024]{1,0:T(8,128)S(1)}) custom-call(s32[2,8]{1,0:T(2,128)S(1)} %bitcast.6, f32[16,1024]{1,0:T(8,128)S(1)} %get-tuple-element.82.s.refs_4_, bf16[8,128,128]{2,1,0:T(8,128)(2,1)S(1)} %get-tuple-element.85.ah, bf16[8,128,128]{2,1,0:T(8,128)(2,1)S(1)} %get-tuple-element.86.al, ...), custom_call_target="tpu_custom_call" | custom-call | flops 1000000000 | bytes 1638464 | tf_op jit(solution)/shard_map/pallas_call | solution.py:371
  66.1 3.0 %collective-permute-done.21.refs_13_ = f32[32,384]{1,0:T(8,128)S(1)} collective-permute-done((f32[32,384]{1,0:T(8,128)S(1)}, f32[32,384]{1,0:T(8,128)S(1)}, u32[]{:S(2)}, u32[]{:S(2)}) %collective-permute-start.21) | collective-permute-done | bytes 49184 | tf_op jit(solution)/shard_map/ppermute | solution.py:541
  69.1 1.7 %shard_map.110 = (f32[2,16,1024]{2,1,0:T(8,128)}, f32[64,128]{1,0:T(8,128)S(1)}) custom-call(s32[2,8]{1,0:T(2,128)S(1)} %bitcast.7, f32[16,1024]{1,0:T(8,128)S(1)} %copy-done, f32[16,1024]{1,0:T(8,128)S(1)} %collective-permute-done.14.refs_1_, f32[16,1024]{1,0:T(8,128)S(1)} %collective-permute-done.15.refs_2_, ...), custom_call_target="tpu_custom_call" | custom-call | flops 1000000000 | bytes 1933376 | tf_op jit(solution)/shard_map/pallas_call | solution.py:371
  70.8 0.9 %collective-permute-start.22 = (f32[64,128]{1,0:T(8,128)S(1)}, f32[64,128]{1,0:T(8,128)S(1)}, u32[]{:S(2)}, u32[]{:S(2)}) collective-permute-start(f32[64,128]{1,0:T(8,128)S(1)} %get-tuple-element.92), channel_id=1, source_target_pairs={{0,4},{4,0},{8,12},{12,8},{16,20},{20,16},{24,28},{28,24},{1,5},{5... | collective-permute-start | bytes 98312 | tf_op jit(solution)/shard_map/ppermute | solution.py:568
  71.8 3.0 %collective-permute-done.22 = f32[64,128]{1,0:T(8,128)S(1)} collective-permute-done((f32[64,128]{1,0:T(8,128)S(1)}, f32[64,128]{1,0:T(8,128)S(1)}, u32[]{:S(2)}, u32[]{:S(2)}) %collective-permute-start.22) | collective-permute-done | bytes 32800 | tf_op jit(solution)/shard_map/ppermute | solution.py:568
  75.2 3.9 %collective-permute-start.25 = (f32[64,128]{1,0:T(8,128)S(1)}, f32[64,128]{1,0:T(8,128)S(1)}, u32[]{:S(2)}, u32[]{:S(2)}) collective-permute-start(f32[64,128]{1,0:T(8,128)S(1)} %add.3.refs_0_), channel_id=1, source_target_pairs={{0,24},{4,28},{8,16},{12,20},{16,8},{20,12},{24,0},{28,4},{1,25},{... | collective-permute-start | bytes 98312 | tf_op jit(solution)/shard_map/ppermute | solution.py:572
  79.2 0.8 %collective-permute-done.24.refs_2_ = f32[64,128]{1,0:T(8,128)S(1)} collective-permute-done((f32[64,128]{1,0:T(8,128)S(1)}, f32[64,128]{1,0:T(8,128)S(1)}, u32[]{:S(2)}, u32[]{:S(2)}) %collective-permute-start.24) | collective-permute-done | bytes 32800 | tf_op jit(solution)/shard_map/ppermute | solution.py:572
  80.0 1.4 %collective-permute-done.25.refs_3_ = f32[64,128]{1,0:T(8,128)S(1)} collective-permute-done((f32[64,128]{1,0:T(8,128)S(1)}, f32[64,128]{1,0:T(8,128)S(1)}, u32[]{:S(2)}, u32[]{:S(2)}) %collective-permute-start.25) | collective-permute-done | bytes 32800 | tf_op jit(solution)/shard_map/ppermute | solution.py:572
  81.4 0.8 shard_map.111
  (43 shorter events, 7.0 us)
Async XLA Ops:
  7.0 11.4 %collective-permute-start.3 = (f32[208,384]{1,0:T(8,128)S(1)}, f32[208,384]{1,0:T(8,128)S(1)}, u32[]{:S(2)}, u32[]{:S(2)}) collective-permute-start(f32[208,384]{1,0:T(8,128)S(1)} %get-tuple-element.50), channel_id=1, source_target_pairs={{0,4},{4,0},{8,12},{12,8},{16,20},{20,16},{24,28},{28,24},{1,5},{5... | collective-permute-start | bytes 958472 | tf_op jit(solution)/shard_map/ppermute | solution.py:433
  11.6 14.4 %collective-permute-start.7 = (f32[208,384]{1,0:T(8,128)S(1)}, f32[208,384]{1,0:T(8,128)S(1)}, u32[]{:S(2)}, u32[]{:S(2)}) collective-permute-start(f32[208,384]{1,0:T(8,128)S(1)} %get-tuple-element.58), channel_id=1, source_target_pairs={{0,4},{4,0},{8,12},{12,8},{16,20},{20,16},{24,28},{28,24},{1,5},{5... | collective-permute-start | bytes 958472 | tf_op jit(solution)/shard_map/ppermute | solution.py:456
  18.5 7.6 %collective-permute-start.4 = (f32[208,384]{1,0:T(8,128)S(1)}, f32[208,384]{1,0:T(8,128)S(1)}, u32[]{:S(2)}, u32[]{:S(2)}) collective-permute-start(f32[208,384]{1,0:T(8,128)S(1)} %collective-permute-done.3.near), channel_id=1, source_target_pairs={{0,1},{1,0},{2,3},{3,2},{4,5},{5,4},{6,7},{7,6},{8,9},{9,8},{10,11... | collective-permute-start | bytes 958472 | tf_op jit(solution)/shard_map/ppermute | solution.py:460
  18.5 5.8 %collective-permute-start = (f32[16,384]{1,0:T(8,128)S(1)}, f32[16,384]{1,0:T(8,128)S(1)}, u32[]{:S(2)}, u32[]{:S(2)}) collective-permute-start(f32[16,384]{1,0:T(8,128)S(1)} %get-tuple-element.48), channel_id=1, source_target_pairs={{0,4},{1,5},{2,6},{3,7}} | collective-permute-start | bytes 73736 | tf_op jit(solution)/shard_map/ppermute | solution.py:432
  24.5 4.7 %copy-start = (f32[16,1024]{1,0:T(8,128)S(1)}, f32[16,1024]{1,0:T(8,128)}, u32[]{:S(2)}) copy-start(f32[16,1024]{1,0:T(8,128)} %refs_0_.1) | copy-start | bytes 196612
  24.5 1.6 %collective-permute-start.1 = (f32[16,384]{1,0:T(8,128)S(1)}, f32[16,384]{1,0:T(8,128)S(1)}, u32[]{:S(2)}, u32[]{:S(2)}) collective-permute-start(f32[16,384]{1,0:T(8,128)S(1)} %shard_map.95), channel_id=1, source_target_pairs={{4,12},{5,13},{6,14},{7,15}} | collective-permute-start | bytes 73736 | tf_op jit(solution)/shard_map/ppermute | solution.py:451
  25.3 0.8 collective-permute-start.2
  26.0 9.3 %collective-permute-start.8 = (f32[208,384]{1,0:T(8,128)S(1)}, f32[208,384]{1,0:T(8,128)S(1)}, u32[]{:S(2)}, u32[]{:S(2)}) collective-permute-start(f32[208,384]{1,0:T(8,128)S(1)} %collective-permute-done.7.near), channel_id=1, source_target_pairs={{0,1},{1,0},{2,3},{3,2},{4,5},{5,4},{6,7},{7,6},{8,9},{9,8},{10,11... | collective-permute-start | bytes 958472 | tf_op jit(solution)/shard_map/ppermute | solution.py:461
  26.8 5.5 %copy-start.1 = (s32[8,2]{0,1:T(2,128)S(1)}, s32[8,2]{0,1:T(2,128)}, u32[]{:S(2)}) copy-start(s32[8,2]{0,1:T(2,128)} %param.13) | copy-start | bytes 196
  27.2 14.0 %collective-permute-start.12 = (f32[192,384]{1,0:T(8,128)S(1)}, f32[192,384]{1,0:T(8,128)S(1)}, u32[]{:S(2)}, u32[]{:S(2)}) collective-permute-start(f32[192,384]{1,0:T(8,128)S(1)} %shard_map.102), channel_id=1, source_target_pairs={{8,0},{12,4},{9,1},{13,5},{10,2},{14,6},{11,3},{15,7}} | collective-permute-start | bytes 884744 | tf_op jit(solution)/shard_map/ppermute | solution.py:467
  28.5 2.7 %collective-permute-start.5 = (f32[16,384]{1,0:T(8,128)S(1)}, f32[16,384]{1,0:T(8,128)S(1)}, u32[]{:S(2)}, u32[]{:S(2)}) collective-permute-start(f32[16,384]{1,0:T(8,128)S(1)} %get-tuple-element.51), channel_id=1, source_target_pairs={{8,16},{12,20},{9,17},{13,21},{10,18},{14,22},{11,19},{15,23}} | collective-permute-start | bytes 73736 | tf_op jit(solution)/shard_map/ppermute | solution.py:474
  29.2 33.9 %collective-permute-start.14 = (f32[16,1024]{1,0:T(8,128)S(1)}, f32[16,1024]{1,0:T(8,128)S(1)}, u32[]{:S(2)}, u32[]{:S(2)}) collective-permute-start(f32[16,1024]{1,0:T(8,128)S(1)} %copy-done), channel_id=1, source_target_pairs={{0,1},{1,0},{2,3},{3,2},{4,5},{5,4},{6,7},{7,6},{8,9},{9,8},{10,11... | collective-permute-start | bytes 196616 | tf_op jit(solution)/shard_map/ppermute | solution.py:389
  29.7 30.1 %collective-permute-start.15 = (f32[16,1024]{1,0:T(8,128)S(1)}, f32[16,1024]{1,0:T(8,128)S(1)}, u32[]{:S(2)}, u32[]{:S(2)}) collective-permute-start(f32[16,1024]{1,0:T(8,128)S(1)} %copy-done), channel_id=1, source_target_pairs={{0,2},{1,3},{2,0},{3,1},{4,6},{5,7},{6,4},{7,5},{8,10},{9,11},{10,... | collective-permute-start | bytes 196616 | tf_op jit(solution)/shard_map/ppermute | solution.py:389
  31.6 3.9 %collective-permute-start.6 = (f32[16,384]{1,0:T(8,128)S(1)}, f32[16,384]{1,0:T(8,128)S(1)}, u32[]{:S(2)}, u32[]{:S(2)}) collective-permute-start(f32[16,384]{1,0:T(8,128)S(1)} %shard_map.97), channel_id=1, source_target_pairs={{16,24},{20,28},{17,25},{21,29},{18,26},{22,30},{19,27},{23,31}} | collective-permute-start | bytes 73736 | tf_op jit(solution)/shard_map/ppermute | solution.py:474
  36.2 10.2 %collective-permute-start.9 = (f32[16,384]{1,0:T(8,128)S(1)}, f32[16,384]{1,0:T(8,128)S(1)}, u32[]{:S(2)}, u32[]{:S(2)}) collective-permute-start(f32[16,384]{1,0:T(8,128)S(1)} %get-tuple-element.62), channel_id=1, source_target_pairs={{24,16},{28,20},{8,0},{12,4},{25,17},{29,21},{9,1},{13,5},{26,18},... | collective-permute-start | bytes 73736 | tf_op jit(solution)/shard_map/ppermute | solution.py:499
  41.2 9.8 %collective-permute-start.13 = (f32[192,384]{1,0:T(8,128)S(1)}, f32[192,384]{1,0:T(8,128)S(1)}, u32[]{:S(2)}, u32[]{:S(2)}) collective-permute-start(f32[192,384]{1,0:T(8,128)S(1)} %collective-permute-done.12.near), channel_id=1, source_target_pairs={{0,1},{1,0},{2,3},{3,2},{4,5},{5,4},{6,7},{7,6},{8,9},{9,8},{10,11... | collective-permute-start | bytes 884744 | tf_op jit(solution)/shard_map/ppermute | solution.py:468
  47.0 4.1 %collective-permute-start.10 = (f32[16,384]{1,0:T(8,128)S(1)}, f32[16,384]{1,0:T(8,128)S(1)}, u32[]{:S(2)}, u32[]{:S(2)}) collective-permute-start(f32[16,384]{1,0:T(8,128)S(1)} %shard_map.101), channel_id=1, source_target_pairs={{16,8},{20,12},{17,9},{21,13},{18,10},{22,14},{19,11},{23,15}} | collective-permute-start | bytes 73736 | tf_op jit(solution)/shard_map/ppermute | solution.py:499
  47.7 8.6 %collective-permute-start.11 = (f32[16,384]{1,0:T(8,128)S(1)}, f32[16,384]{1,0:T(8,128)S(1)}, u32[]{:S(2)}, u32[]{:S(2)}) collective-permute-start(f32[16,384]{1,0:T(8,128)S(1)} %shard_map.101), channel_id=1, source_target_pairs={{16,0},{20,4},{17,1},{21,5},{18,2},{22,6},{19,3},{23,7}} | collective-permute-start | bytes 73736 | tf_op jit(solution)/shard_map/ppermute | solution.py:493
  58.3 6.1 %collective-permute-start.18 = (f32[16,1024]{1,0:T(8,128)S(1)}, f32[16,1024]{1,0:T(8,128)S(1)}, u32[]{:S(2)}, u32[]{:S(2)}) collective-permute-start(f32[16,1024]{1,0:T(8,128)S(1)} %get-tuple-element.82.s.refs_4_), channel_id=1, source_target_pairs={{0,2},{1,3},{2,0},{3,1},{4,6},{5,7},{6,4},{7,5},{8,10},{9,11},{10,... | collective-permute-start | bytes 196616 | tf_op jit(solution)/shard_map/ppermute | solution.py:389
  59.8 6.3 %collective-permute-start.16 = (f32[16,1024]{1,0:T(8,128)S(1)}, f32[16,1024]{1,0:T(8,128)S(1)}, u32[]{:S(2)}, u32[]{:S(2)}) collective-permute-start(f32[16,1024]{1,0:T(8,128)S(1)} %collective-permute-done.15.refs_2_), channel_id=1, source_target_pairs={{0,1},{1,0},{2,3},{3,2},{4,5},{5,4},{6,7},{7,6},{8,9},{9,8},{10,11... | collective-permute-start | bytes 196616 | tf_op jit(solution)/shard_map/ppermute | solution.py:389
  59.8 9.3 %collective-permute-start.17 = (f32[16,1024]{1,0:T(8,128)S(1)}, f32[16,1024]{1,0:T(8,128)S(1)}, u32[]{:S(2)}, u32[]{:S(2)}) collective-permute-start(f32[16,1024]{1,0:T(8,128)S(1)} %get-tuple-element.82.s.refs_4_), channel_id=1, source_target_pairs={{0,1},{1,0},{2,3},{3,2},{4,5},{5,4},{6,7},{7,6},{8,9},{9,8},{10,11... | collective-permute-start | bytes 196616 | tf_op jit(solution)/shard_map/ppermute | solution.py:389
  60.3 5.8 %collective-permute-start.20 = (f32[32,384]{1,0:T(8,128)S(1)}, f32[32,384]{1,0:T(8,128)S(1)}, u32[]{:S(2)}, u32[]{:S(2)}) collective-permute-start(f32[32,384]{1,0:T(8,128)S(1)} %get-tuple-element.89), channel_id=1, source_target_pairs={{0,4},{4,8},{8,12},{12,16},{16,20},{20,24},{24,28},{1,5},{5,9},{9,... | collective-permute-start | bytes 147464 | tf_op jit(solution)/shard_map/ppermute | solution.py:540
  63.1 6.0 %collective-permute-start.21 = (f32[32,384]{1,0:T(8,128)S(1)}, f32[32,384]{1,0:T(8,128)S(1)}, u32[]{:S(2)}, u32[]{:S(2)}) collective-permute-start(f32[32,384]{1,0:T(8,128)S(1)} %get-tuple-element.90), channel_id=1, source_target_pairs={{4,0},{8,4},{12,8},{16,12},{20,16},{24,20},{28,24},{5,1},{9,5},{13... | collective-permute-start | bytes 147464 | tf_op jit(solution)/shard_map/ppermute | solution.py:541
  64.4 4.7 %collective-permute-start.19 = (f32[16,1024]{1,0:T(8,128)S(1)}, f32[16,1024]{1,0:T(8,128)S(1)}, u32[]{:S(2)}, u32[]{:S(2)}) collective-permute-start(f32[16,1024]{1,0:T(8,128)S(1)} %collective-permute-done.18.refs_6_), channel_id=1, source_target_pairs={{0,1},{1,0},{2,3},{3,2},{4,5},{5,4},{6,7},{7,6},{8,9},{9,8},{10,11... | collective-permute-start | bytes 196616 | tf_op jit(solution)/shard_map/ppermute | solution.py:389
  70.8 3.9 %collective-permute-start.22 = (f32[64,128]{1,0:T(8,128)S(1)}, f32[64,128]{1,0:T(8,128)S(1)}, u32[]{:S(2)}, u32[]{:S(2)}) collective-permute-start(f32[64,128]{1,0:T(8,128)S(1)} %get-tuple-element.92), channel_id=1, source_target_pairs={{0,4},{4,0},{8,12},{12,8},{16,20},{20,16},{24,28},{28,24},{1,5},{5... | collective-permute-start | bytes 98312 | tf_op jit(solution)/shard_map/ppermute | solution.py:568
  74.8 4.4 %collective-permute-start.23 = (f32[64,128]{1,0:T(8,128)S(1)}, f32[64,128]{1,0:T(8,128)S(1)}, u32[]{:S(2)}, u32[]{:S(2)}) collective-permute-start(f32[64,128]{1,0:T(8,128)S(1)} %add.3.refs_0_), channel_id=1, source_target_pairs={{0,8},{4,12},{8,0},{12,4},{16,24},{20,28},{24,16},{28,20},{1,9},{5... | collective-permute-start | bytes 98312 | tf_op jit(solution)/shard_map/ppermute | solution.py:572
  75.2 4.8 %collective-permute-start.24 = (f32[64,128]{1,0:T(8,128)S(1)}, f32[64,128]{1,0:T(8,128)S(1)}, u32[]{:S(2)}, u32[]{:S(2)}) collective-permute-start(f32[64,128]{1,0:T(8,128)S(1)} %add.3.refs_0_), channel_id=1, source_target_pairs={{0,16},{4,20},{8,24},{12,28},{16,0},{20,4},{24,8},{28,12},{1,17},{... | collective-permute-start | bytes 98312 | tf_op jit(solution)/shard_map/ppermute | solution.py:572
  75.2 6.2 %collective-permute-start.25 = (f32[64,128]{1,0:T(8,128)S(1)}, f32[64,128]{1,0:T(8,128)S(1)}, u32[]{:S(2)}, u32[]{:S(2)}) collective-permute-start(f32[64,128]{1,0:T(8,128)S(1)} %add.3.refs_0_), channel_id=1, source_target_pairs={{0,24},{4,28},{8,16},{12,20},{16,8},{20,12},{24,0},{28,4},{1,25},{... | collective-permute-start | bytes 98312 | tf_op jit(solution)/shard_map/ppermute | solution.py:572

commit v2 on v1

--- a/solution.py
+++ b/solution.py
@@ -235,8 +235,8 @@
 def solve_kernel(n, offs, *refs):
     got, rest = refs[:n], refs[n:]
     (skip, ph, plow, high, low, e, va, kha, kla, vb, khb, klb, oh, ol, x, belowx) = rest[:16]
-    (w, inner, tail, below, push) = rest[16:]
-    width, size = x.shape
+    (w, inner, inside, across, push) = rest[16:]
+    _, size = x.shape
     odd = lax.rem(lax.axis_index("slab"), 2) == 1
     u_in = total(got) + dot3(split(skip[...]), (ph[...], plow[...]), NT)
     u_mid = e[1] + step_rows(u_in, high, low, 1, NT)
@@ -250,13 +250,12 @@
     )
     w[...] = solved
     inner[...] = solved
-    tail[:width] = x[:, size - TAIL :]
-    tail[width:] = solved[:, size - TAIL :]
     front = [solved[:, i * BS : (i + 1) * BS] for i in range(BW)]
     push_head(offs, front, oh, ol, push)
-    below[:width] = belowx[...]
-    for j in range(BW):
-        below[width:, j * BS : (j + 1) * BS] = push[j]
+    tail = jnp.concatenate([x[:, size - TAIL :], solved[:, size - TAIL :]], 0)
+    below = jnp.concatenate([belowx[...], lanes([push[j] for j in range(BW)])], 0)
+    inside[...] = jnp.where(odd, below, tail)
+    across[...] = jnp.where(odd, tail, below)
 
 
 def band_local(offs, s, ah, al, oh, ol, ext, acc, img, imt):
@@ -319,10 +318,13 @@
 
 def gram_kernel(count, nodes, offs, *refs):
     xs, ws = refs[:count], refs[count : 2 * count]
-    (imgx, imtx, imgw, imtw, head, above, oh, ol, image, gram, left, right, hb) = refs[2 * count :]
+    (imgx, imtx, imgw, imtw, inside, across, oh, ol, image, gram, left, right, hb) = refs[2 * count :]
     width = xs[0].shape[0]
     size = xs[0].shape[1]
     me = lax.axis_index("col")
+    odd = lax.rem(lax.axis_index("slab"), 2) == 1
+    head = jnp.where(odd, inside[...], across[...])
+    above = jnp.where(odd, across[...], inside[...])
     for j in range(BW):
         hb[j] = head[:, j * BS : (j + 1) * BS]
         hb[BW + j] = jnp.zeros((2 * width, BS), F32)
@@ -455,8 +457,6 @@
     )
     n_near = lax.ppermute(ndh, "slab", near)
     x_all = gathered(vectors, "col")
-    up = [(i, i + 1) for i in range(slabs - 1)]
-    down = [(i + 1, i) for i in range(slabs - 1)]
     m_other = lax.ppermute(m_near, "col", cores)
     n_other = lax.ppermute(n_near, "col", cores)
 
@@ -526,7 +526,7 @@
         flops=2 * 10**9,
     )
     halo = ((2 * width, TAIL), F32)
-    w, inner, tail, below = call(
+    w, inner, inside, across = call(
         last_kernel,
         [flat, flat, halo, halo],
         [offsets]
@@ -537,8 +537,9 @@
         flops=4 * 10**8,
     )
     w_all = gathered(inner, "col")
-    head = lax.ppermute(tail, "slab", up)
-    above = lax.ppermute(below, "slab", down)
+    inside = lax.ppermute(inside, "slab", near)
+    between = [(i, i + 1) for i in range(1, slabs - 1, 2)]
+    across = lax.ppermute(across, "slab", between + [(j, i) for i, j in between])
     imgw, imtw = call(
         band_w_kernel,
         [flat, flat],
@@ -553,7 +554,7 @@
         [offsets]
         + x_all
         + w_all
-        + [imgx, imtx, imgw, imtw, head, above, oh, ol],
+        + [imgx, imtx, imgw, imtw, inside, across, oh, ol],
         smem=1,
         scratch=[
             pltpu.VMEM((4 * width, size), F32),

time: 82.5 us -> 81 us (0.982)
  waiting for transfers between devices: 28.3 us -> 25.5 us
  starting transfers between devices: 28 us -> 29.2 us
    ppermute x1, starting transfers between devices: 0.91 us -> 4.79 us  [local_program(): gram = gram + lax.ppermute(gram, 'slab', links)]
    ppermute x2, waiting for transfers between devices: 3.01 us -> 0.25 us  [the longest x1 0.25 us: local_program(): inside = lax.ppermute(inside, 'slab', near)]
    ppermute x2, starting transfers between devices: 4.09 us -> 1.56 us  [the longest x1 0.9 us: local_program(): inside = lax.ppermute(inside, 'slab', near)]
    ppermute x1, waiting for transfers between devices: 3 us -> 1.89 us  [local_program(): gram = gram + lax.ppermute(gram, 'slab', links)]
  transfers between devices with their start and end apart: 26 -> 26, of which waited for: 9 -> 10; matrix products, arithmetic and copies ran while one was open for 0% -> 0% of each run, Pallas kernels for 20% -> 20%
where the time goes in v2:
time: 81 us; the launch traced here: 80.7 us
  starting transfers between devices  29.2 us (36%)
  waiting for transfers between devices  25.5 us (31%)
  Pallas kernels  24.9 us (31%)
  between operations  0.91 us (1%)
    pallas_call x18, Pallas kernels, call(): pl.pallas_call(kernel, out_shape=shapes, in_specs=specs, out_specs=[pl.Bl...  24.9 us
    ppermute x1, waiting for transfers between devices, local_program(): m_near = lax.ppermute(mch, 'slab', near)  6.82 us
    ppermute x1, waiting for transfers between devices, local_program(): skip = lax.ppermute(u_out, 'slab', [(4, 0), (5, 1)])  5.11 us
    ppermute x1, starting transfers between devices, local_program(): gram = gram + lax.ppermute(gram, 'slab', links)  4.79 us
    ppermute x3, starting transfers between devices, local_program(): lax.ppermute(gram, 'slab', [(i, i ^ far) for i in range(slabs)])  4.39 us
    ppermute x6, starting transfers between devices, gathered(): parts[k ^ step] = lax.ppermute(parts[k], axis, links)  4.03 us
    ppermute x1, starting transfers between devices, local_program(): c_got = lax.ppermute(c_own, 'slab', [(0, 1)])  3.91 us
    ppermute x2, waiting for transfers between devices, local_program(): got.append(lax.ppermute(u_out, 'slab', hop))  3.09 us
  transfers between devices with their start and end apart: 26, of which 10 were waited for; matrix products, arithmetic and copies ran while one was open for 0% of the time, Pallas kernels for 20%

profile of v2, /device:TPU:0, one launch (start us, length us, event | category | flops | bytes accessed | tf_op | source)
XLA Modules:
  0.0 80.7 jit_solution(5012293466073244044)
XLA Ops:
  0.6 6.4 %shard_map.94 = (f32[400,384]{1,0:T(8,128)S(1)}, f32[208,384]{1,0:T(8,128)S(1)}, f32[16,384]{1,0:T(8,128)S(1)}, f32[8,16,128]{2,1,0:T(8,128)S(1)}, bf16[11,400,1...) custom-call(s32[2,8]{1,0:T(2,128)} %bitcast.1, ...), custom_call_target="tpu_custom_call" | custom-call | flops 4000000000 | bytes 1638464 | tf_op jit(solution)/shard_map/pallas_call | solution.py:373
  7.0 3.1 %collective-permute-start.3 = (f32[208,384]{1,0:T(8,128)S(1)}, f32[208,384]{1,0:T(8,128)S(1)}, u32[]{:S(2)}, u32[]{:S(2)}) collective-permute-start(f32[208,384]{1,0:T(8,128)S(1)} %get-tuple-element.50), channel_id=1, source_target_pairs={{0,4},{4,0},{8,12},{12,8},{16,20},{20,16},{24,28},{28,24},{1,5},{5... | collective-permute-start | bytes 958472 | tf_op jit(solution)/shard_map/ppermute | solution.py:435
  10.1 1.5 %shard_map.98 = (f32[400,384]{1,0:T(8,128)S(1)}, f32[208,384]{1,0:T(8,128)S(1)}) custom-call(bf16[11,400,128]{2,1,0:T(8,128)(2,1)S(1)} %get-tuple-element.55.fh.refs_7_, bf16[11,400,128]{2,1,0:T(8,128)(2,1)S(1)} %get-tuple-element.56.fl.refs_8_), custom_call_target="tpu_custom_call" | custom-call | flops 1000000000 | bytes 2252800 | tf_op jit(solution)/shard_map/pallas_call | solution.py:373
  11.7 6.8 %collective-permute-done.3.near = f32[208,384]{1,0:T(8,128)S(1)} collective-permute-done((f32[208,384]{1,0:T(8,128)S(1)}, f32[208,384]{1,0:T(8,128)S(1)}, u32[]{:S(2)}, u32[]{:S(2)}) %collective-permute-start.3) | collective-permute-done | bytes 319520 | tf_op jit(solution)/shard_map/ppermute | solution.py:435
  18.5 3.9 %collective-permute-start = (f32[16,384]{1,0:T(8,128)S(1)}, f32[16,384]{1,0:T(8,128)S(1)}, u32[]{:S(2)}, u32[]{:S(2)}) collective-permute-start(f32[16,384]{1,0:T(8,128)S(1)} %get-tuple-element.48), channel_id=1, source_target_pairs={{0,4},{1,5},{2,6},{3,7}} | collective-permute-start | bytes 73736 | tf_op jit(solution)/shard_map/ppermute | solution.py:434
  22.4 1.9 %collective-permute-done.c_got = f32[16,384]{1,0:T(8,128)S(1)} collective-permute-done((f32[16,384]{1,0:T(8,128)S(1)}, f32[16,384]{1,0:T(8,128)S(1)}, u32[]{:S(2)}, u32[]{:S(2)}) %collective-permute-start) | collective-permute-done | bytes 24608 | tf_op jit(solution)/shard_map/ppermute | solution.py:434
  24.5 0.8 collective-permute-start.1
  27.2 1.3 %collective-permute-start.12 = (f32[192,384]{1,0:T(8,128)S(1)}, f32[192,384]{1,0:T(8,128)S(1)}, u32[]{:S(2)}, u32[]{:S(2)}) collective-permute-start(f32[192,384]{1,0:T(8,128)S(1)} %shard_map.102), channel_id=1, source_target_pairs={{8,0},{12,4},{9,1},{13,5},{10,2},{14,6},{11,3},{15,7}} | collective-permute-start | bytes 884744 | tf_op jit(solution)/shard_map/ppermute | solution.py:467
  29.7 1.5 %collective-permute-start.15 = (f32[16,1024]{1,0:T(8,128)S(1)}, f32[16,1024]{1,0:T(8,128)S(1)}, u32[]{:S(2)}, u32[]{:S(2)}) collective-permute-start(f32[16,1024]{1,0:T(8,128)S(1)} %copy-done), channel_id=1, source_target_pairs={{0,2},{1,3},{2,0},{3,1},{4,6},{5,7},{6,4},{7,5},{8,10},{9,11},{10,... | collective-permute-start | bytes 196616 | tf_op jit(solution)/shard_map/ppermute | solution.py:391
  32.3 3.0 %shard_map.107 = (f32[16,1024]{1,0:T(8,128)S(1)}, f32[16,1024]{1,0:T(8,128)S(1)}, f32[16,384]{1,0:T(8,128)S(1)}, bf16[8,128,128]{2,1,0:T(8,128)(2,1)S(1)}, bf16[...) custom-call(s32[2,8]{1,0:T(2,128)S(1)} %bitcast.2, ...), custom_call_target="tpu_custom_call" | custom-call | flops 1000000000 | bytes 1638464 | tf_op jit(solution)/shard_map/pallas_call | solution.py:373
  35.5 0.7 shard_map.100
  36.2 1.3 %collective-permute-start.9 = (f32[16,384]{1,0:T(8,128)S(1)}, f32[16,384]{1,0:T(8,128)S(1)}, u32[]{:S(2)}, u32[]{:S(2)}) collective-permute-start(f32[16,384]{1,0:T(8,128)S(1)} %get-tuple-element.62), channel_id=1, source_target_pairs={{24,16},{28,20},{8,0},{12,4},{25,17},{29,21},{9,1},{13,5},{26,18},... | collective-permute-start | bytes 73736 | tf_op jit(solution)/shard_map/ppermute | solution.py:499
  38.1 3.1 %collective-permute-done.12.near = f32[192,384]{1,0:T(8,128)S(1)} collective-permute-done((f32[192,384]{1,0:T(8,128)S(1)}, f32[192,384]{1,0:T(8,128)S(1)}, u32[]{:S(2)}, u32[]{:S(2)}) %collective-permute-start.12) | collective-permute-done | bytes 294944 | tf_op jit(solution)/shard_map/ppermute | solution.py:467
  41.2 2.1 %shard_map.105 = (f32[11,400,128]{2,1,0:T(8,128)S(1)}, bf16[384,512]{1,0:T(8,128)(2,1)S(1)}, bf16[384,512]{1,0:T(8,128)(2,1)S(1)}, f32[16,512]{1,0:T(8,128)S(1)}) custom-call(s32[2,8]{1,0:T(2,128)S(1)} %bitcast.3, f32[8,16,128]{2,1,0:T(8,128)S(1)} %shard_map.104.z, bf16[8,128,128]{2,1,0:T(8,128)(2,1)S(1)} %get-tuple-element.67.dh, ...), custom_call_target="tpu_custom_call" | custom-call | flops 2000000000 | bytes 1638464 | tf_op jit(solution)/shard_map/pallas_call | solution.py:373
  43.3 3.1 %collective-permute-done.9.refs_0_ = f32[16,384]{1,0:T(8,128)S(1)} collective-permute-done((f32[16,384]{1,0:T(8,128)S(1)}, f32[16,384]{1,0:T(8,128)S(1)}, u32[]{:S(2)}, u32[]{:S(2)}) %collective-permute-start.9) | collective-permute-done | bytes 24608 | tf_op jit(solution)/shard_map/ppermute | solution.py:499
  47.0 0.7 collective-permute-start.10
  47.7 1.3 %collective-permute-start.11 = (f32[16,384]{1,0:T(8,128)S(1)}, f32[16,384]{1,0:T(8,128)S(1)}, u32[]{:S(2)}, u32[]{:S(2)}) collective-permute-start(f32[16,384]{1,0:T(8,128)S(1)} %shard_map.101), channel_id=1, source_target_pairs={{16,0},{20,4},{17,1},{21,5},{18,2},{22,6},{19,3},{23,7}} | collective-permute-start | bytes 73736 | tf_op jit(solution)/shard_map/ppermute | solution.py:493
  49.0 2.0 %shard_map.106 = (bf16[384,512]{1,0:T(8,128)(2,1)S(1)}, bf16[384,512]{1,0:T(8,128)(2,1)S(1)}, f32[16,512]{1,0:T(8,128)S(1)}) custom-call(s32[2,8]{1,0:T(2,128)S(1)} %bitcast.4, f32[11,400,128]{2,1,0:T(8,128)S(1)} %get-tuple-element.74.q_in, bf16[8,128,128]{2,1,0:T(8,128)(2,1)S(1)} %get-tuple-element.67.dh, bf16[8,128,128]{2,1,0:T(8,128)(2,1)S(1)} %get-tuple-element.68.dl, ...), custom_call_target="tpu_custom_call" | custom-call | flops 2000000000 | bytes 3825728 | tf_op jit(solution)/shard_map/pallas_call | solution.py:373
  51.1 5.1 %collective-permute-done.11.refs_2_ = f32[16,384]{1,0:T(8,128)S(1)} collective-permute-done((f32[16,384]{1,0:T(8,128)S(1)}, f32[16,384]{1,0:T(8,128)S(1)}, u32[]{:S(2)}, u32[]{:S(2)}) %collective-permute-start.11) | collective-permute-done | bytes 24608 | tf_op jit(solution)/shard_map/ppermute | solution.py:493
  56.2 2.0 %shard_map.108 = (f32[16,1024]{1,0:T(8,128)}, f32[16,1024]{1,0:T(8,128)S(1)}, f32[32,384]{1,0:T(8,128)S(1)}, f32[32,384]{1,0:T(8,128)S(1)}) custom-call(s32[2,8]{1,0:T(2,128)S(1)} %bitcast.5, f32[16,384]{1,0:T(8,128)S(1)} %collective-permute-done.9.refs_0_, f32[16,384]{1,0:T(8,128)S(1)} %collective-permute-done.10.refs_1_, ...), custom_call_target="tpu_custom_call" | custom-call | flops 400000000 | bytes 4669504 | tf_op jit(solution)/shard_map/pallas_call | solution.py:373
  58.3 1.5 %collective-permute-start.18 = (f32[16,1024]{1,0:T(8,128)S(1)}, f32[16,1024]{1,0:T(8,128)S(1)}, u32[]{:S(2)}, u32[]{:S(2)}) collective-permute-start(f32[16,1024]{1,0:T(8,128)S(1)} %get-tuple-element.82.s.refs_4_), channel_id=1, source_target_pairs={{0,2},{1,3},{2,0},{3,1},{4,6},{5,7},{6,4},{7,5},{8,10},{9,11},{10,... | collective-permute-start | bytes 196616 | tf_op jit(solution)/shard_map/ppermute | solution.py:391
  60.3 0.9 %collective-permute-start.20 = (f32[32,384]{1,0:T(8,128)S(1)}, f32[32,384]{1,0:T(8,128)S(1)}, u32[]{:S(2)}, u32[]{:S(2)}) collective-permute-start(f32[32,384]{1,0:T(8,128)S(1)} %get-tuple-element.89), channel_id=1, source_target_pairs={{0,4},{4,0},{8,12},{12,8},{16,20},{20,16},{24,28},{28,24},{1,5},{5... | collective-permute-start | bytes 147464 | tf_op jit(solution)/shard_map/ppermute | solution.py:540
  61.9 0.7 collective-permute-done.18.refs_6_
  62.6 1.6 %shard_map.109 = (f32[16,1024]{1,0:T(8,128)S(1)}, f32[16,1024]{1,0:T(8,128)S(1)}) custom-call(s32[2,8]{1,0:T(2,128)S(1)} %bitcast.6, f32[16,1024]{1,0:T(8,128)S(1)} %get-tuple-element.82.s.refs_4_, bf16[8,128,128]{2,1,0:T(8,128)(2,1)S(1)} %get-tuple-element.85.ah, bf16[8,128,128]{2,1,0:T(8,128)(2,1)S(1)} %get-tuple-element.86.al, ...), custom_call_target="tpu_custom_call" | custom-call | flops 1000000000 | bytes 1638464 | tf_op jit(solution)/shard_map/pallas_call | solution.py:373
  64.4 1.7 %shard_map.110 = (f32[2,16,1024]{2,1,0:T(8,128)}, f32[64,128]{1,0:T(8,128)S(1)}) custom-call(s32[2,8]{1,0:T(2,128)S(1)} %bitcast.7, f32[16,1024]{1,0:T(8,128)S(1)} %copy-done, f32[16,1024]{1,0:T(8,128)S(1)} %collective-permute-done.14.refs_1_, f32[16,1024]{1,0:T(8,128)S(1)} %collective-permute-done.15.refs_2_, ...), custom_call_target="tpu_custom_call" | custom-call | flops 1000000000 | bytes 1933376 | tf_op jit(solution)/shard_map/pallas_call | solution.py:373
  66.1 4.8 %collective-permute-start.22 = (f32[64,128]{1,0:T(8,128)S(1)}, f32[64,128]{1,0:T(8,128)S(1)}, u32[]{:S(2)}, u32[]{:S(2)}) collective-permute-start(f32[64,128]{1,0:T(8,128)S(1)} %get-tuple-element.92), channel_id=1, source_target_pairs={{0,4},{4,0},{8,12},{12,8},{16,20},{20,16},{24,28},{28,24},{1,5},{5... | collective-permute-start | bytes 98312 | tf_op jit(solution)/shard_map/ppermute | solution.py:569
  70.9 1.9 %collective-permute-done.22 = f32[64,128]{1,0:T(8,128)S(1)} collective-permute-done((f32[64,128]{1,0:T(8,128)S(1)}, f32[64,128]{1,0:T(8,128)S(1)}, u32[]{:S(2)}, u32[]{:S(2)}) %collective-permute-start.22) | collective-permute-done | bytes 32800 | tf_op jit(solution)/shard_map/ppermute | solution.py:569
  73.4 0.8 collective-permute-start.24
  74.2 3.0 %collective-permute-start.25 = (f32[64,128]{1,0:T(8,128)S(1)}, f32[64,128]{1,0:T(8,128)S(1)}, u32[]{:S(2)}, u32[]{:S(2)}) collective-permute-start(f32[64,128]{1,0:T(8,128)S(1)} %add.3.refs_0_), channel_id=1, source_target_pairs={{0,24},{4,28},{8,16},{12,20},{16,8},{20,12},{24,0},{28,4},{1,25},{... | collective-permute-start | bytes 98312 | tf_op jit(solution)/shard_map/ppermute | solution.py:573
  77.2 1.0 %collective-permute-done.24.refs_2_ = f32[64,128]{1,0:T(8,128)S(1)} collective-permute-done((f32[64,128]{1,0:T(8,128)S(1)}, f32[64,128]{1,0:T(8,128)S(1)}, u32[]{:S(2)}, u32[]{:S(2)}) %collective-permute-start.24) | collective-permute-done | bytes 32800 | tf_op jit(solution)/shard_map/ppermute | solution.py:573
  78.2 1.7 %collective-permute-done.25.refs_3_ = f32[64,128]{1,0:T(8,128)S(1)} collective-permute-done((f32[64,128]{1,0:T(8,128)S(1)}, f32[64,128]{1,0:T(8,128)S(1)}, u32[]{:S(2)}, u32[]{:S(2)}) %collective-permute-start.25) | collective-permute-done | bytes 32800 | tf_op jit(solution)/shard_map/ppermute | solution.py:573
  79.9 0.8 shard_map.111
  (43 shorter events, 7.9 us)
Async XLA Ops:
  7.0 11.4 %collective-permute-start.3 = (f32[208,384]{1,0:T(8,128)S(1)}, f32[208,384]{1,0:T(8,128)S(1)}, u32[]{:S(2)}, u32[]{:S(2)}) collective-permute-start(f32[208,384]{1,0:T(8,128)S(1)} %get-tuple-element.50), channel_id=1, source_target_pairs={{0,4},{4,0},{8,12},{12,8},{16,20},{20,16},{24,28},{28,24},{1,5},{5... | collective-permute-start | bytes 958472 | tf_op jit(solution)/shard_map/ppermute | solution.py:435
  11.6 14.4 %collective-permute-start.7 = (f32[208,384]{1,0:T(8,128)S(1)}, f32[208,384]{1,0:T(8,128)S(1)}, u32[]{:S(2)}, u32[]{:S(2)}) collective-permute-start(f32[208,384]{1,0:T(8,128)S(1)} %get-tuple-element.58), channel_id=1, source_target_pairs={{0,4},{4,0},{8,12},{12,8},{16,20},{20,16},{24,28},{28,24},{1,5},{5... | collective-permute-start | bytes 958472 | tf_op jit(solution)/shard_map/ppermute | solution.py:458
  18.5 7.6 %collective-permute-start.4 = (f32[208,384]{1,0:T(8,128)S(1)}, f32[208,384]{1,0:T(8,128)S(1)}, u32[]{:S(2)}, u32[]{:S(2)}) collective-permute-start(f32[208,384]{1,0:T(8,128)S(1)} %collective-permute-done.3.near), channel_id=1, source_target_pairs={{0,1},{1,0},{2,3},{3,2},{4,5},{5,4},{6,7},{7,6},{8,9},{9,8},{10,11... | collective-permute-start | bytes 958472 | tf_op jit(solution)/shard_map/ppermute | solution.py:460
  18.5 5.8 %collective-permute-start = (f32[16,384]{1,0:T(8,128)S(1)}, f32[16,384]{1,0:T(8,128)S(1)}, u32[]{:S(2)}, u32[]{:S(2)}) collective-permute-start(f32[16,384]{1,0:T(8,128)S(1)} %get-tuple-element.48), channel_id=1, source_target_pairs={{0,4},{1,5},{2,6},{3,7}} | collective-permute-start | bytes 73736 | tf_op jit(solution)/shard_map/ppermute | solution.py:434
  24.5 4.7 %copy-start = (f32[16,1024]{1,0:T(8,128)S(1)}, f32[16,1024]{1,0:T(8,128)}, u32[]{:S(2)}) copy-start(f32[16,1024]{1,0:T(8,128)} %refs_0_.1) | copy-start | bytes 196612
  24.5 1.6 %collective-permute-start.1 = (f32[16,384]{1,0:T(8,128)S(1)}, f32[16,384]{1,0:T(8,128)S(1)}, u32[]{:S(2)}, u32[]{:S(2)}) collective-permute-start(f32[16,384]{1,0:T(8,128)S(1)} %shard_map.95), channel_id=1, source_target_pairs={{4,12},{5,13},{6,14},{7,15}} | collective-permute-start | bytes 73736 | tf_op jit(solution)/shard_map/ppermute | solution.py:453
  25.3 0.8 collective-permute-start.2
  26.0 9.3 %collective-permute-start.8 = (f32[208,384]{1,0:T(8,128)S(1)}, f32[208,384]{1,0:T(8,128)S(1)}, u32[]{:S(2)}, u32[]{:S(2)}) collective-permute-start(f32[208,384]{1,0:T(8,128)S(1)} %collective-permute-done.7.near), channel_id=1, source_target_pairs={{0,1},{1,0},{2,3},{3,2},{4,5},{5,4},{6,7},{7,6},{8,9},{9,8},{10,11... | collective-permute-start | bytes 958472 | tf_op jit(solution)/shard_map/ppermute | solution.py:461
  26.8 5.5 %copy-start.1 = (s32[8,2]{0,1:T(2,128)S(1)}, s32[8,2]{0,1:T(2,128)}, u32[]{:S(2)}) copy-start(s32[8,2]{0,1:T(2,128)} %param.13) | copy-start | bytes 196
  27.2 14.0 %collective-permute-start.12 = (f32[192,384]{1,0:T(8,128)S(1)}, f32[192,384]{1,0:T(8,128)S(1)}, u32[]{:S(2)}, u32[]{:S(2)}) collective-permute-start(f32[192,384]{1,0:T(8,128)S(1)} %shard_map.102), channel_id=1, source_target_pairs={{8,0},{12,4},{9,1},{13,5},{10,2},{14,6},{11,3},{15,7}} | collective-permute-start | bytes 884744 | tf_op jit(solution)/shard_map/ppermute | solution.py:467
  28.5 2.7 %collective-permute-start.5 = (f32[16,384]{1,0:T(8,128)S(1)}, f32[16,384]{1,0:T(8,128)S(1)}, u32[]{:S(2)}, u32[]{:S(2)}) collective-permute-start(f32[16,384]{1,0:T(8,128)S(1)} %get-tuple-element.51), channel_id=1, source_target_pairs={{8,16},{12,20},{9,17},{13,21},{10,18},{14,22},{11,19},{15,23}} | collective-permute-start | bytes 73736 | tf_op jit(solution)/shard_map/ppermute | solution.py:474
  29.2 32.0 %collective-permute-start.14 = (f32[16,1024]{1,0:T(8,128)S(1)}, f32[16,1024]{1,0:T(8,128)S(1)}, u32[]{:S(2)}, u32[]{:S(2)}) collective-permute-start(f32[16,1024]{1,0:T(8,128)S(1)} %copy-done), channel_id=1, source_target_pairs={{0,1},{1,0},{2,3},{3,2},{4,5},{5,4},{6,7},{7,6},{8,9},{9,8},{10,11... | collective-permute-start | bytes 196616 | tf_op jit(solution)/shard_map/ppermute | solution.py:391
  29.7 30.1 %collective-permute-start.15 = (f32[16,1024]{1,0:T(8,128)S(1)}, f32[16,1024]{1,0:T(8,128)S(1)}, u32[]{:S(2)}, u32[]{:S(2)}) collective-permute-start(f32[16,1024]{1,0:T(8,128)S(1)} %copy-done), channel_id=1, source_target_pairs={{0,2},{1,3},{2,0},{3,1},{4,6},{5,7},{6,4},{7,5},{8,10},{9,11},{10,... | collective-permute-start | bytes 196616 | tf_op jit(solution)/shard_map/ppermute | solution.py:391
  31.6 3.9 %collective-permute-start.6 = (f32[16,384]{1,0:T(8,128)S(1)}, f32[16,384]{1,0:T(8,128)S(1)}, u32[]{:S(2)}, u32[]{:S(2)}) collective-permute-start(f32[16,384]{1,0:T(8,128)S(1)} %shard_map.97), channel_id=1, source_target_pairs={{16,24},{20,28},{17,25},{21,29},{18,26},{22,30},{19,27},{23,31}} | collective-permute-start | bytes 73736 | tf_op jit(solution)/shard_map/ppermute | solution.py:474
  36.2 10.2 %collective-permute-start.9 = (f32[16,384]{1,0:T(8,128)S(1)}, f32[16,384]{1,0:T(8,128)S(1)}, u32[]{:S(2)}, u32[]{:S(2)}) collective-permute-start(f32[16,384]{1,0:T(8,128)S(1)} %get-tuple-element.62), channel_id=1, source_target_pairs={{24,16},{28,20},{8,0},{12,4},{25,17},{29,21},{9,1},{13,5},{26,18},... | collective-permute-start | bytes 73736 | tf_op jit(solution)/shard_map/ppermute | solution.py:499
  41.2 9.8 %collective-permute-start.13 = (f32[192,384]{1,0:T(8,128)S(1)}, f32[192,384]{1,0:T(8,128)S(1)}, u32[]{:S(2)}, u32[]{:S(2)}) collective-permute-start(f32[192,384]{1,0:T(8,128)S(1)} %collective-permute-done.12.near), channel_id=1, source_target_pairs={{0,1},{1,0},{2,3},{3,2},{4,5},{5,4},{6,7},{7,6},{8,9},{9,8},{10,11... | collective-permute-start | bytes 884744 | tf_op jit(solution)/shard_map/ppermute | solution.py:468
  47.0 4.1 %collective-permute-start.10 = (f32[16,384]{1,0:T(8,128)S(1)}, f32[16,384]{1,0:T(8,128)S(1)}, u32[]{:S(2)}, u32[]{:S(2)}) collective-permute-start(f32[16,384]{1,0:T(8,128)S(1)} %shard_map.101), channel_id=1, source_target_pairs={{16,8},{20,12},{17,9},{21,13},{18,10},{22,14},{19,11},{23,15}} | collective-permute-start | bytes 73736 | tf_op jit(solution)/shard_map/ppermute | solution.py:499
  47.7 8.6 %collective-permute-start.11 = (f32[16,384]{1,0:T(8,128)S(1)}, f32[16,384]{1,0:T(8,128)S(1)}, u32[]{:S(2)}, u32[]{:S(2)}) collective-permute-start(f32[16,384]{1,0:T(8,128)S(1)} %shard_map.101), channel_id=1, source_target_pairs={{16,0},{20,4},{17,1},{21,5},{18,2},{22,6},{19,3},{23,7}} | collective-permute-start | bytes 73736 | tf_op jit(solution)/shard_map/ppermute | solution.py:493
  58.3 4.3 %collective-permute-start.18 = (f32[16,1024]{1,0:T(8,128)S(1)}, f32[16,1024]{1,0:T(8,128)S(1)}, u32[]{:S(2)}, u32[]{:S(2)}) collective-permute-start(f32[16,1024]{1,0:T(8,128)S(1)} %get-tuple-element.82.s.refs_4_), channel_id=1, source_target_pairs={{0,2},{1,3},{2,0},{3,1},{4,6},{5,7},{6,4},{7,5},{8,10},{9,11},{10,... | collective-permute-start | bytes 196616 | tf_op jit(solution)/shard_map/ppermute | solution.py:391
  59.8 4.3 %collective-permute-start.16 = (f32[16,1024]{1,0:T(8,128)S(1)}, f32[16,1024]{1,0:T(8,128)S(1)}, u32[]{:S(2)}, u32[]{:S(2)}) collective-permute-start(f32[16,1024]{1,0:T(8,128)S(1)} %collective-permute-done.15.refs_2_), channel_id=1, source_target_pairs={{0,1},{1,0},{2,3},{3,2},{4,5},{5,4},{6,7},{7,6},{8,9},{9,8},{10,11... | collective-permute-start | bytes 196616 | tf_op jit(solution)/shard_map/ppermute | solution.py:391
  59.8 4.6 %collective-permute-start.17 = (f32[16,1024]{1,0:T(8,128)S(1)}, f32[16,1024]{1,0:T(8,128)S(1)}, u32[]{:S(2)}, u32[]{:S(2)}) collective-permute-start(f32[16,1024]{1,0:T(8,128)S(1)} %get-tuple-element.82.s.refs_4_), channel_id=1, source_target_pairs={{0,1},{1,0},{2,3},{3,2},{4,5},{5,4},{6,7},{7,6},{8,9},{9,8},{10,11... | collective-permute-start | bytes 196616 | tf_op jit(solution)/shard_map/ppermute | solution.py:391
  60.3 4.1 %collective-permute-start.20 = (f32[32,384]{1,0:T(8,128)S(1)}, f32[32,384]{1,0:T(8,128)S(1)}, u32[]{:S(2)}, u32[]{:S(2)}) collective-permute-start(f32[32,384]{1,0:T(8,128)S(1)} %get-tuple-element.89), channel_id=1, source_target_pairs={{0,4},{4,0},{8,12},{12,8},{16,20},{20,16},{24,28},{28,24},{1,5},{5... | collective-permute-start | bytes 147464 | tf_op jit(solution)/shard_map/ppermute | solution.py:540
  61.2 3.2 %collective-permute-start.21 = (f32[32,384]{1,0:T(8,128)S(1)}, f32[32,384]{1,0:T(8,128)S(1)}, u32[]{:S(2)}, u32[]{:S(2)}) collective-permute-start(f32[32,384]{1,0:T(8,128)S(1)} %get-tuple-element.90), channel_id=1, source_target_pairs={{4,8},{12,16},{20,24},{8,4},{16,12},{24,20},{5,9},{13,17},{21,25},... | collective-permute-start | bytes 147464 | tf_op jit(solution)/shard_map/ppermute | solution.py:542
  62.6 1.8 %collective-permute-start.19 = (f32[16,1024]{1,0:T(8,128)S(1)}, f32[16,1024]{1,0:T(8,128)S(1)}, u32[]{:S(2)}, u32[]{:S(2)}) collective-permute-start(f32[16,1024]{1,0:T(8,128)S(1)} %collective-permute-done.18.refs_6_), channel_id=1, source_target_pairs={{0,1},{1,0},{2,3},{3,2},{4,5},{5,4},{6,7},{7,6},{8,9},{9,8},{10,11... | collective-permute-start | bytes 196616 | tf_op jit(solution)/shard_map/ppermute | solution.py:391
  66.1 6.7 %collective-permute-start.22 = (f32[64,128]{1,0:T(8,128)S(1)}, f32[64,128]{1,0:T(8,128)S(1)}, u32[]{:S(2)}, u32[]{:S(2)}) collective-permute-start(f32[64,128]{1,0:T(8,128)S(1)} %get-tuple-element.92), channel_id=1, source_target_pairs={{0,4},{4,0},{8,12},{12,8},{16,20},{20,16},{24,28},{28,24},{1,5},{5... | collective-permute-start | bytes 98312 | tf_op jit(solution)/shard_map/ppermute | solution.py:569
  72.8 4.4 %collective-permute-start.23 = (f32[64,128]{1,0:T(8,128)S(1)}, f32[64,128]{1,0:T(8,128)S(1)}, u32[]{:S(2)}, u32[]{:S(2)}) collective-permute-start(f32[64,128]{1,0:T(8,128)S(1)} %add.3.refs_0_), channel_id=1, source_target_pairs={{0,8},{4,12},{8,0},{12,4},{16,24},{20,28},{24,16},{28,20},{1,9},{5... | collective-permute-start | bytes 98312 | tf_op jit(solution)/shard_map/ppermute | solution.py:573
  73.4 4.8 %collective-permute-start.24 = (f32[64,128]{1,0:T(8,128)S(1)}, f32[64,128]{1,0:T(8,128)S(1)}, u32[]{:S(2)}, u32[]{:S(2)}) collective-permute-start(f32[64,128]{1,0:T(8,128)S(1)} %add.3.refs_0_), channel_id=1, source_target_pairs={{0,16},{4,20},{8,24},{12,28},{16,0},{20,4},{24,8},{28,12},{1,17},{... | collective-permute-start | bytes 98312 | tf_op jit(solution)/shard_map/ppermute | solution.py:573
  74.2 5.7 %collective-permute-start.25 = (f32[64,128]{1,0:T(8,128)S(1)}, f32[64,128]{1,0:T(8,128)S(1)}, u32[]{:S(2)}, u32[]{:S(2)}) collective-permute-start(f32[64,128]{1,0:T(8,128)S(1)} %add.3.refs_0_), channel_id=1, source_target_pairs={{0,24},{4,28},{8,16},{12,20},{16,8},{20,12},{24,0},{28,4},{1,25},{... | collective-permute-start | bytes 98312 | tf_op jit(solution)/shard_map/ppermute | solution.py:573
